TPU v7x, 512 devices: a whole 4x4x16 slice. The times are simulated.
512 devices in a mesh: dp: 8 (over x, core), seq: 64 (over y, z).
Axes of the slice: x: 4, y: 4, z: 16, core: 2. Of those that a mesh axis runs over, the one named last changes fastest.
Arguments:
- inputs: float32 [8, 8192, 128], P('dp', 'seq'), parts along dimension 0, may hold values from -48 to 48
- trajectory: float32 [8, 8192, 128], P('dp', 'seq'), parts along dimension 0, may hold values from -0.9 to 0.9
- initial_state: float32 [8, 128], P('dp'), parts along dimension 0, may hold values from -0.9 to 0.9
- cotangent: float32 [8, 8192, 128], P('dp', 'seq'), parts along dimension 0, may hold values from -1 to 1
- in_weight: float32 [128, 384], replicated, may hold values from -0.5 to 0.5
- recurrent_weight: float32 [128, 384], replicated, may hold values from -0.5 to 0.5
- gate_bias: float32 [384], replicated
Outputs:
- new_state: float32 [8, 8192, 128], P('dp', 'seq'), parts along dimension 0
- adjoint: float32 [8, 8192, 128], P('dp', 'seq'), parts along dimension 0
There are 8 independent parts, one for each index of `dp`. A program takes and returns all parts, laid end to end along the dimension named above; an argument that names none is the same for every part. Nothing has to cross between parts.
All inputs are finite; a program needn't handle non-finite values.
Results may differ from a plain program's by a relative error of at most 0.0003.
Values sent between devices are 32-bit elements; how exact they have to be, the bound alone decides.
No kernel may reach another device: no remote copies, remote signals or barrier semaphores. Data moves between devices by JAX's collectives and lax.ppermute only.
A program may use at most 64 MiB of HBM per device.

v0:
```python
import jax
import jax.numpy as jnp
from jax import lax
from jax.sharding import PartitionSpec as P

BLOCK = 16


HIGHEST_PRECISION = lax.Precision.HIGHEST


def passed_along(value, axis, steps):
    count = lax.axis_size(axis)
    leading, last = (max(0, -steps), min(count, count - steps))
    return lax.ppermute(value, axis, [(source, source + steps) for source in range(leading, last)])


def prefix(part, axis, combine, identity, reverse):
    count = lax.axis_size(axis)
    place = lax.axis_index(axis)
    ahead = count - 1 - place if reverse else place
    gathered = jax.tree.map(lambda a: lax.all_gather(a, axis), part)
    state = jax.tree.map(lambda a, e: jnp.zeros_like(a) + jnp.asarray(e, a.dtype), part, identity)

    def one(turn, state):
        source = count - 1 - turn if reverse else turn
        return combine(
            state, jax.tree.map(lambda a: lax.dynamic_index_in_dim(a, source, 0, False), gathered)
        )

    return lax.fori_loop(0, ahead, one, state)


def sum_parts(tensor, hidden_width):
    return (
        tensor[..., :hidden_width]
        + tensor[..., hidden_width : 2 * hidden_width]
        + tensor[..., 2 * hidden_width :]
    )


def linearize(features, previous, in_weight, recurrent_weight, gate_bias):
    hidden_width = previous.shape[-1]
    projected = (
        jnp.dot(
            features, in_weight, precision=HIGHEST_PRECISION, preferred_element_type=jnp.float32
        )
        + gate_bias
    )
    recurrent = jnp.dot(
        previous, recurrent_weight, precision=HIGHEST_PRECISION, preferred_element_type=jnp.float32
    )
    reset_gate = jax.nn.sigmoid(projected[:, :hidden_width] + recurrent[:, :hidden_width])
    write_gate = jax.nn.sigmoid(
        projected[:, hidden_width : 2 * hidden_width]
        + recurrent[:, hidden_width : 2 * hidden_width]
    )
    cand_recurrent = recurrent[:, 2 * hidden_width :]
    candidate = jnp.tanh(projected[:, 2 * hidden_width :] + reset_gate * cand_recurrent)
    updated = previous + write_gate * (candidate - previous)
    keep_rate = 1.0 - write_gate
    slopes = write_gate * (1.0 - candidate * candidate)
    gate_terms = jnp.concatenate(
        [
            slopes * cand_recurrent * reset_gate * (1.0 - reset_gate),
            (candidate - previous) * write_gate * (1.0 - write_gate),
            slopes * reset_gate,
        ],
        axis=1,
    )
    offsets = updated - keep_rate * previous - sum_parts(gate_terms * recurrent, hidden_width)
    return (keep_rate, gate_terms, offsets)


def apply_jacobian(keep_rate, gate_terms, vector, recurrent_weight):
    hidden_width = vector.shape[-1]
    mapped = jnp.einsum("bk,kj->bj", vector, recurrent_weight, precision=HIGHEST_PRECISION)
    return keep_rate * vector + sum_parts(gate_terms * mapped, hidden_width)


def apply_transposed(keep_rate, gate_terms, vector, recurrent_weight):
    tiled = jnp.concatenate([vector, vector, vector], axis=-1)
    return keep_rate * vector + jnp.einsum(
        "bk,jk->bj", gate_terms * tiled, recurrent_weight, precision=HIGHEST_PRECISION
    )


def jacobians(keep_rate, gate_terms, weight_parts):
    hidden_width = keep_rate.shape[-1]
    coupling = gate_terms[:, :hidden_width, None] * weight_parts[0][None]
    coupling = (
        coupling + gate_terms[:, hidden_width : 2 * hidden_width, None] * weight_parts[1][None]
    )
    coupling = coupling + gate_terms[:, 2 * hidden_width :, None] * weight_parts[2][None]
    return coupling + keep_rate[:, :, None] * jnp.eye(hidden_width, dtype=jnp.float32)


def matvec(matrix, vector):
    return jnp.einsum("...ij,...j->...i", matrix, vector, precision=HIGHEST_PRECISION)


def compose(earlier, later):
    return (
        jnp.matmul(later[0], earlier[0], precision=HIGHEST_PRECISION),
        matvec(later[0], earlier[1]) + later[1],
    )


def per_device(
    inputs, trajectory, initial_state, cotangent, in_weight, recurrent_weight, gate_bias
):
    tok_rows = trajectory.shape[1]
    hidden_width = trajectory.shape[2]
    position = lax.axis_index("seq")
    boundary_row = passed_along(trajectory[:, tok_rows - 1, :], "seq", 1)
    first_row = jnp.where(position == 0, initial_state, boundary_row)
    previous = jnp.concatenate([first_row, trajectory[0, : tok_rows - 1]], axis=0)
    keep_rate, gate_terms, offsets = linearize(
        inputs[0], previous, in_weight, recurrent_weight, gate_bias
    )
    blocks = tok_rows // BLOCK
    weight_parts = jnp.transpose(recurrent_weight.reshape(hidden_width, 3, hidden_width), (1, 2, 0))

    def by_step(tensor):
        return tensor.reshape(blocks, BLOCK, tensor.shape[-1]).swapaxes(0, 1)

    keep_steps = by_step(keep_rate)
    term_steps = by_step(gate_terms)
    offset_steps = by_step(offsets)
    cotan_steps = by_step(cotangent[0])
    identity = jnp.broadcast_to(
        jnp.eye(hidden_width, dtype=jnp.float32), (blocks, hidden_width, hidden_width)
    )
    zero_rows = jnp.zeros((blocks, hidden_width), jnp.float32)

    def gather_segment(carried, step_items):
        product, forward_sum, adjoint_sum = carried
        keep_now, terms_now, offset_now, cotan_now = step_items
        forward_sum = forward_sum + matvec(product, offset_now)
        costate = cotan_now + adjoint_sum
        adjoint_sum = apply_transposed(keep_now, terms_now, costate, recurrent_weight)
        product = jnp.matmul(
            product, jacobians(keep_now, terms_now, weight_parts), precision=HIGHEST_PRECISION
        )
        return ((product, forward_sum, adjoint_sum), None)

    (composite, block_offset, block_adjoint), _ = lax.scan(
        gather_segment,
        (identity, zero_rows, zero_rows),
        (keep_steps, term_steps, offset_steps, cotan_steps),
        reverse=True,
    )
    forward_maps = lax.associative_scan(compose, (composite, block_offset), axis=0)
    reverse_maps = lax.associative_scan(
        compose, (jnp.swapaxes(composite, 1, 2)[::-1], block_adjoint[::-1]), axis=0
    )
    device_matrix = forward_maps[0][blocks - 1]
    device_offset = forward_maps[1][blocks - 1]
    device_adjoint = reverse_maps[1][blocks - 1]
    start_state = initial_state[0]
    eye_matrix = jnp.eye(hidden_width, dtype=jnp.float32)
    zero_vector = jnp.zeros((hidden_width,), jnp.float32)
    prefix_matrix, prefix_offset = prefix(
        (device_matrix, device_offset), "seq", compose, (eye_matrix, zero_vector), False
    )
    entry_state = matvec(prefix_matrix, start_state) + prefix_offset
    suffix_matrix, entry_adjoint = prefix(
        (reverse_maps[0][blocks - 1], device_adjoint),
        "seq",
        compose,
        (eye_matrix, zero_vector),
        True,
    )
    block_exit = matvec(forward_maps[0], entry_state) + forward_maps[1]
    block_entry = jnp.concatenate([entry_state[None], block_exit[: blocks - 1]], axis=0)
    reverse_out = (matvec(reverse_maps[0], entry_adjoint) + reverse_maps[1])[::-1]
    block_incoming = jnp.concatenate([reverse_out[1:], entry_adjoint[None]], axis=0)

    def forward_apply(hidden_state, step_items):
        keep_now, terms_now, offset_now = step_items
        hidden_state = (
            apply_jacobian(keep_now, terms_now, hidden_state, recurrent_weight) + offset_now
        )
        return (hidden_state, hidden_state)

    _, states = lax.scan(forward_apply, block_entry, (keep_steps, term_steps, offset_steps))

    def backward_apply(carried, step_items):
        keep_now, terms_now, cotan_now = step_items
        costate = cotan_now + carried
        carried = apply_transposed(keep_now, terms_now, costate, recurrent_weight)
        return (carried, costate)

    _, adjoint_rows = lax.scan(
        backward_apply, block_incoming, (keep_steps, term_steps, cotan_steps), reverse=True
    )
    new_state = states.swapaxes(0, 1).reshape(1, tok_rows, hidden_width)
    adjoint = adjoint_rows.swapaxes(0, 1).reshape(1, tok_rows, hidden_width)
    return (new_state, adjoint)


def solution(mesh):
    return jax.shard_map(
        per_device,
        mesh=mesh,
        in_specs=(
            P("dp", "seq", None),
            P("dp", "seq", None),
            P("dp", None),
            P("dp", "seq", None),
            P(),
            P(),
            P(),
        ),
        out_specs=(P("dp", "seq", None), P("dp", "seq", None)),
        check_vma=False,
    )
```

profile of v0, /device:TPU:504, one launch (start us, length us, event | category | flops | bytes accessed | tf_op | source)
XLA Modules:
  0.0 511.3 jit_solution(17915020233778316667)
XLA Ops:
  8.0 1.3 collective-permute-start
  10.2 1.2 convolution_add_fusion.2
  12.3 1.1 copy.38
  13.6 1.2 fusion.98
  15.2 28.2 %while.77 = (s32[]{:T(128)}, f32[8,128,128]{1,2,0:T(8,128)S(1)}, f32[8,128]{1,0:T(8,128)S(1)}, f32[8,128]{1,0:T(8,128)S(1)}, f32[16,8,384]{2,1,0:T(8,128)S(1)}, ...) while((s32[]{:T(128)}, f32[8,128,128]{1,2,0:T(8,128)S(1)}, ...), condition=%wide.region_1.2_spmd.clone, body=%wide.region_0.1_spmd.clone.sunk | while | flops 208583680 | bytes 3678371 | solution.py:147
  52.9 71.9 %all-gather.1 = f32[64,1,128]{2,1,0:T(1,128)S(1)} all-gather(f32[1,1,128]{2,1,0:T(1,128)S(1)} %slice_bitcast_fusion.18), channel_id=1, replica_groups=mesh['dp'=8,'seq'=64] {'seq'}, dimensions={0}, use_global_device_ids=true | all-gather | bytes 33280 | tf_op jit(solution)/shard_map/all_gather | solution.py:22
  124.8 72.0 %all-gather = f32[64,1,128]{2,1,0:T(1,128)S(1)} all-gather(f32[1,1,128]{2,1,0:T(1,128)S(1)} %slice_bitcast_fusion.19), channel_id=1, replica_groups=mesh['dp'=8,'seq'=64] {'seq'}, dimensions={0}, use_global_device_ids=true | all-gather | bytes 33280 | tf_op jit(solution)/shard_map/all_gather | solution.py:22
  198.2 16.6 %while.76 = (s32[]{:T(128)}, f32[8,128]{1,0:T(8,128)S(1)}, f32[16,8,128]{2,1,0:T(8,128)S(1)}, f32[16,8,128]{2,1,0:T(8,128)S(1)}, f32[16,8,128]{2,1,0:T(8,128)S(1...) while((s32[]{:T(128)}, f32[8,128]{1,0:T(8,128)S(1)}, ...), condition=%wide.region_9.10_spmd, body=%wide.region_8.9_spmd.sunk | while | flops 4730883 | bytes 242797 | solution.py:194
  215.5 125.0 %all-gather.5.cloned.1.call-done = f32[64,128,128]{2,1,0:T(8,128)} async-done(((f32[1,128,128]{2,1,0:T(8,128)}), f32[64,128,128]{2,1,0:T(8,128)}) %all-gather.5.cloned.1.call-update) | async-done | bytes 4194320 | tf_op jit(solution)/shard_map/all_gather | solution.py:22
  340.5 136.5 %while.73 = (s32[]{:T(128)}, f32[128,128]{1,0:T(8,128)S(1)}, f32[128]{0:T(128)S(1)}, s32[]{:T(128)}, f32[64,128,128]{2,1,0:T(8,128)}, /*index=5*/f32[64,128]{1,0:T(8,128)S(1)}, s32[]{:T(128)}, s32[]{:T(128)}, s32[]{:T(128)}) while((s32[]{:T(128)}, f32[128,128]{1,0:T(8,128)S(1)}, f32[128]{0:T(128)S(1)}, s32[]{:T(128)}, ...), condition=%wide.region_3.4_spmd, body=%wide.region_2.3_spmd.sunk | while | flops 25362564 | bytes 396931 | solution.py:31
  341.5 1.0 fusion.170
  345.9 1.0 fusion.170
  348.1 1.0 fusion.170
  352.4 1.0 fusion.170
  354.6 1.0 fusion.170
  356.7 1.0 fusion.170
  361.1 1.0 fusion.170
  363.2 1.0 fusion.170
  365.4 1.0 fusion.170
  367.6 1.0 fusion.170
  369.7 1.0 fusion.170
  371.9 1.0 fusion.170
  374.1 1.0 fusion.170
  376.2 1.0 fusion.170
  378.4 1.0 fusion.170
  380.6 1.0 fusion.170
  382.7 1.0 fusion.170
  384.9 1.0 fusion.170
  387.1 1.0 fusion.170
  389.2 1.0 fusion.170
  393.6 1.0 fusion.170
  395.7 1.0 fusion.170
  397.9 1.0 fusion.170
  402.2 1.0 fusion.170
  404.4 1.0 fusion.170
  408.8 1.0 fusion.170
  410.9 1.0 fusion.170
  413.1 1.0 fusion.170
  415.3 1.0 fusion.170
  417.4 1.0 fusion.170
  419.6 1.0 fusion.170
  421.8 1.0 fusion.170
  423.9 1.0 fusion.170
  426.1 1.0 fusion.170
  428.3 1.0 fusion.170
  430.4 1.0 fusion.170
  432.6 1.0 fusion.170
  434.8 1.0 fusion.170
  436.9 1.0 fusion.170
  439.1 1.0 fusion.170
  443.4 1.0 fusion.170
  445.6 1.0 fusion.170
  447.8 1.0 fusion.170
  452.1 1.0 fusion.170
  454.3 1.0 fusion.170
  458.6 1.0 fusion.170
  460.8 1.0 fusion.170
  462.9 1.0 fusion.170
  465.1 1.0 fusion.170
  467.3 1.0 fusion.170
  469.4 1.0 fusion.170
  471.6 1.0 fusion.170
  473.8 1.0 fusion.170
  477.9 26.0 %while.74 = (s32[]{:T(128)}, f32[8,128]{1,0:T(8,128)S(1)}, f32[16,8,128]{2,1,0:T(8,128)S(1)}, f32[16,8,128]{2,1,0:T(8,128)S(1)}, f32[16,8,384]{2,1,0:T(8,128)}, ...) while((s32[]{:T(128)}, f32[8,128]{1,0:T(8,128)S(1)}, f32[16,8,128]{2,1,0:T(8,128)S(1)}, ...), condition=%wide.region_5.6_spmd, body=%wide.region_4.5_spmd.sunk | while | flops 4726786 | bytes 258141 | solution.py:186
  (583 shorter events, 163.0 us)
Async XLA Ops:
  7.2 3.0 copy-start
  7.2 8.0 %copy-start.1 = (f32[128,384]{1,0:T(8,128)S(1)}, f32[128,384]{1,0:T(8,128)}, u32[]{:S(2)}) copy-start(f32[128,384]{1,0:T(8,128)} %param.22) | copy-start | bytes 589828
  7.2 190.3 %all-gather.7.cloned.1.call-start = ((), (), s32[]{:S(2)}) async-start(), calls=%async_computation.1 | async-start | bytes 4259840 | tf_op jit(solution)/shard_map/all_gather | solution.py:22
  8.0 5.5 %collective-permute-start = (f32[1,128]{1,0:T(1,128)S(1)}, f32[1,128]{1,0:T(1,128)S(1)}, u32[]{:S(2)}, u32[]{:S(2)}) collective-permute-start(f32[1,128]{1,0:T(1,128)S(1)} %slice_bitcast_fusion.20), channel_id=1, source_target_pairs={{0,1},{1,2},{2,3},{3,4},{4,5},{5,6},{6,7},{7,8},{8,9},{9,10},{10,1... | collective-permute-start | bytes 1544 | tf_op jit(solution)/shard_map/ppermute | solution.py:15
  43.4 0.8 copy-start.2
  43.4 0.8 copy-start.3
  46.8 293.7 %all-gather.5.cloned.1.call-start = ((), (), s32[]{:S(2)}) async-start(), calls=%async_computation | async-start | bytes 4259840 | tf_op jit(solution)/shard_map/all_gather | solution.py:22
  52.4 424.7 %copy-start.4 = (f32[1,128]{1,0:T(1,128)S(1)}, f32[1,128]{1,0:T(1,128)}, u32[]{:S(2)}) copy-start(f32[1,128]{1,0:T(1,128)} %param.19) | copy-start | bytes 1540
Sparse Core Ops, SparseCore 0:
  46.9 143.1 all-gather.6
  197.6 142.8 all-gather.4
where the time goes:
time: 519 us; the launch traced here: 511 us
  matrix products  195 us (38%)
  blocking collectives  144 us (28%)
  waiting for transfers between devices  125 us (24%)
  between operations  14.7 us (3%)
  other arithmetic  14.2 us (3%)
  local copies, waits for them, and re-layouts  12.4 us (2%)
    all_gather x2, blocking collectives, prefix(): gathered = jax.tree.map(lambda a: lax.all_gather(a, axis), part)  144 us
    all_gather x2, waiting for transfers between devices, prefix(): gathered = jax.tree.map(lambda a: lax.all_gather(a, axis), part)  125 us
    dot_general x92, matrix products, matvec(): jnp.einsum('...ij,...j->...i', matrix, vector, precision=HIGHEST_PRECISION)  77.3 us
    dot_general x73, matrix products, compose(): jnp.matmul(later[0], earlier[0], precision=HIGHEST_PRECISION)  68.9 us
    dot_general x32, matrix products, apply_transposed(): jnp.einsum('bk,jk->bj', gate_terms * tiled, recurrent_weight, precision=H...  19.6 us
    dot_general x16, matrix products, apply_jacobian(): jnp.einsum('bk,kj->bj', vector, recurrent_weight, precision=HIGHEST_PRECI...  14.8 us
    dot_general x16, matrix products, gather_segment(): jnp.matmul(product, jacobians(keep_now, terms_now, weight_parts), precisi...  12.3 us
    dynamic_update_slice x32, other arithmetic, per_device(): lax.scan(forward_apply, block_entry, (keep_steps, term_steps, offset_steps))  11.8 us
  transfers between devices with their start and end apart: 3, of which 1 were waited for; matrix products, arithmetic and copies ran while one was open for 6% of the time, Pallas kernels for 0%

commit v1 on v0

v1 whole, which is shorter than its diff:
```python
import jax
import jax.numpy as jnp
from jax import lax
from jax.experimental import pallas as pl
from jax.experimental.pallas import tpu as pltpu
from jax.sharding import PartitionSpec as P

F32 = jnp.float32
BF16 = jnp.bfloat16
H = 128
BLOCKS = 16
ROW_B = 128
ROW_C = 129
ROW_PROJ = 130
ROW_REC = 133
ROW_LAST = 136
ROWS = 144
VMEM_LIMIT = 48 * 1024 * 1024


def split(x):
    hi = x.astype(BF16)
    return hi, (x - hi.astype(F32)).astype(BF16)


def left(x):
    return jnp.concatenate(split(x), axis=1)


def right(x):
    row = jnp.concatenate(split(x), axis=1)
    return jnp.concatenate([row, row], axis=0)


def right_t(x):
    hi, lo = split(x)
    return jnp.concatenate(
        [jnp.concatenate([hi, hi], axis=1), jnp.concatenate([lo, lo], axis=1)], axis=0
    )


def both_halves(out):
    half = out.shape[1] // 2
    return out[:, :half] + out[:, half:]


def mm(a, b):
    return both_halves(jnp.dot(left(a), right(b), preferred_element_type=F32))


def mm_t(a, b):
    return both_halves(
        lax.dot_general(
            left(a), right_t(b), (((1,), (1,)), ((), ())), preferred_element_type=F32
        )
    )


def pad8(row):
    return jnp.broadcast_to(row, (8, H))


def vec_mm(row, b):
    return mm(pad8(row), b)[:1]


def vec_mm_t(row, b):
    return mm_t(pad8(row), b)[:1]


def eye():
    rows = lax.broadcasted_iota(jnp.int32, (H, H), 0)
    cols = lax.broadcasted_iota(jnp.int32, (H, H), 1)
    return (rows == cols).astype(F32)


def gates(proj, rec, prev):
    reset = jax.nn.sigmoid(proj[0] + rec[0])
    write = jax.nn.sigmoid(proj[1] + rec[1])
    cand = jnp.tanh(proj[2] + reset * rec[2])
    slope = write * (1.0 - cand * cand)
    terms = (
        slope * rec[2] * reset * (1.0 - reset),
        (cand - prev) * write * (1.0 - write),
        slope * reset,
    )
    off = write * cand - (terms[0] * rec[0] + terms[1] * rec[1] + terms[2] * rec[2])
    return write, terms, off


def parts3(x):
    return x[:, :H], x[:, H : 2 * H], x[:, 2 * H :]


def leaf(u, write, terms, ident):
    return u[0] * terms[0] + u[1] * terms[1] + u[2] * terms[2] - ident * write


def compose(early, late):
    lb, lv, lc = early
    rb, rv, rc = late
    prod = mm(jnp.concatenate([lb, pad8(lv)], axis=0), rb)
    return (
        lb + rb + prod[:H],
        lv + rv + prod[H : H + 1],
        lc + rc + vec_mm_t(rc, lb),
    )


def local_kernel(
    x_ref,
    traj_ref,
    cot_ref,
    init_ref,
    win_ref,
    wrec_ref,
    bias_ref,
    pack_ref,
    nodes_ref,
    vecs_ref,
    steps_ref,
    recinit_ref,
):
    traj = traj_ref[0]
    proj = (
        jnp.dot(x_ref[0], win_ref[...], precision=lax.Precision.HIGHEST, preferred_element_type=F32)
        + bias_ref[...]
    )
    rec_in = jnp.concatenate([traj, pad8(init_ref[...])], axis=0)
    rec_all = jnp.dot(
        rec_in, wrec_ref[...], precision=lax.Precision.HIGHEST, preferred_element_type=F32
    )
    recinit_ref[...] = rec_all[H : H + 1]
    rec_rows = rec_all[:H]
    rec = pltpu.roll(rec_rows, 1, 0)
    prev = pltpu.roll(traj, 1, 0)
    write, terms, off = gates(parts3(proj), parts3(rec), prev)
    inner = lax.broadcasted_iota(jnp.int32, (H, H), 0) > 0
    write = jnp.where(inner, write, 0.0)
    terms = [jnp.where(inner, t, 0.0) for t in terms]
    off = jnp.where(inner, off, 0.0)
    for p, rows in enumerate((*terms, write, off)):
        steps_ref[p] = rows

    ident = eye()
    per_block = H // BLOCKS

    def one_block(k, carry):
        base = pl.multiple_of(k * per_block, per_block)
        rows = [steps_ref[p, pl.ds(base, per_block), :] for p in range(4)]
        u = [wrec_ref[:, p * H : (p + 1) * H] for p in range(3)]
        maps = []
        for l in range(per_block):
            row = [r[l : l + 1] for r in rows]
            maps.append(leaf(u, row[3], row[:3], ident))
        while len(maps) > 1:
            maps = [
                maps[i] + maps[i + 1] + mm(maps[i], maps[i + 1]) for i in range(0, len(maps), 2)
            ]
        nodes_ref[BLOCKS + k] = maps[0]
        return carry

    lax.fori_loop(0, BLOCKS, one_block, 0)

    u_right, u_right_t = weights_of(wrec_ref)
    fwd = jnp.zeros((BLOCKS, H), F32)
    bwd = jnp.zeros((BLOCKS, H), F32)
    for l in range(per_block):
        fwd = forward_step(fwd, steps_ref, l, u_right, per_block)
        _, bwd = backward_step(bwd, steps_ref, cot_ref, per_block - 1 - l, u_right_t, per_block)
    vecs_ref[BLOCKS : 2 * BLOCKS, :H] = fwd
    vecs_ref[BLOCKS : 2 * BLOCKS, H:] = bwd

    def node(n):
        return nodes_ref[n], vecs_ref[n : n + 1, :H], vecs_ref[n : n + 1, H:]

    for n in range(BLOCKS - 1, 0, -1):
        m, v, c = compose(node(2 * n), node(2 * n + 1))
        nodes_ref[n] = m
        vecs_ref[n : n + 1, :H] = v
        vecs_ref[n : n + 1, H:] = c
    nodes_ref[0] = jnp.zeros((H, H), F32)
    vecs_ref[0:1, :] = jnp.zeros((1, 2 * H), F32)
    m, v, c = node(1)
    rec_last = rec_rows[H - 1 : H]
    write_pack(
        pack_ref,
        m,
        [v, c]
        + [proj[0:1, p * H : (p + 1) * H] for p in range(3)]
        + [rec_last[:, p * H : (p + 1) * H] for p in range(3)]
        + [traj[H - 1 : H]],
    )


def write_pack(pack_ref, m, rows):
    tail = jnp.concatenate(rows + [jnp.zeros((ROWS - H - len(rows), H), F32)], axis=0)
    for i in range(pack_ref.shape[0]):
        pack_ref[i, :H] = m
        pack_ref[i, H:] = tail


def weights_of(wrec_ref):
    u = wrec_ref[...]
    return right(u), right_t(u)


def every(ref, l, per_block):
    return ref[pl.ds(l, BLOCKS, stride=per_block), :]


def forward_step(h, steps_ref, l, u_right, per_block):
    term = [every(steps_ref.at[p], l, per_block) for p in range(5)]
    mapped = parts3(both_halves(jnp.dot(left(h), u_right, preferred_element_type=F32)))
    moved = term[0] * mapped[0] + term[1] * mapped[1] + term[2] * mapped[2]
    return h + (moved - term[3] * h) + term[4]


def backward_step(carried, steps_ref, cot_ref, l, u_right_t, per_block):
    term = [every(steps_ref.at[p], l, per_block) for p in range(4)]
    costate = carried + every(cot_ref.at[0], l, per_block)
    scaled = jnp.concatenate([term[p] * costate for p in range(3)], axis=1)
    back = both_halves(
        lax.dot_general(
            left(scaled), u_right_t, (((1,), (1,)), ((), ())), preferred_element_type=F32
        )
    )
    return costate, costate + (back - term[3] * costate)


def boundaries(group_ref, wrec_ref, ident):
    u = [wrec_ref[:, p * H : (p + 1) * H] for p in range(3)]
    found = []
    for j in range(1, 4):
        proj = [group_ref[j, ROW_PROJ + p : ROW_PROJ + p + 1] for p in range(3)]
        rec = [group_ref[j - 1, ROW_REC + p : ROW_REC + p + 1] for p in range(3)]
        write, terms, off = gates(proj, rec, group_ref[j - 1, ROW_LAST : ROW_LAST + 1])
        found.append((leaf(u, write, terms, ident), off))
    return found


def links(group_ref, wrec_ref):
    ident = eye()
    firsts = boundaries(group_ref, wrec_ref, ident)
    ahead, behind = [], []
    for j in range(3):
        first, off = firsts[j]
        part = group_ref[j, :H]
        prod = mm(group_ref[j, : H + 8], first)
        ahead.append(
            (
                part + first + prod[:H],
                group_ref[j, ROW_B : ROW_B + 1] + off + prod[ROW_B : ROW_B + 1],
            )
        )
        part = group_ref[j + 1, :H]
        cc = group_ref[j + 1, ROW_C : ROW_C + 1]
        prod = mm(jnp.concatenate([first, pad8(off)], axis=0), part)
        behind.append(
            (
                part + first + prod[:H],
                off + prod[H : H + 1] + group_ref[j + 1, ROW_B : ROW_B + 1],
                cc + vec_mm_t(cc, first),
            )
        )
    return ahead, behind


def merge_kernel(group_ref, wrec_ref, pack_ref, ahead_ref, behind_ref):
    ahead, behind = links(group_ref, wrec_ref)
    for j in range(3):
        m, v = ahead[j]
        ahead_ref[j, :H] = m
        ahead_ref[j, H:] = pad8(v)
        m, v, c = behind[j]
        behind_ref[j, :H] = m
        behind_ref[j, H:] = pad8(c)
    start = (
        group_ref[0, :H],
        group_ref[0, ROW_B : ROW_B + 1],
        group_ref[0, ROW_C : ROW_C + 1],
    )
    m, v, c = compose(compose(start, behind[0]), compose(behind[1], behind[2]))
    write_pack(
        pack_ref,
        m,
        [v, c]
        + [group_ref[0, ROW_PROJ + p : ROW_PROJ + p + 1] for p in range(3)]
        + [group_ref[3, ROW_REC + p : ROW_REC + p + 1] for p in range(3)]
        + [group_ref[3, ROW_LAST : ROW_LAST + 1]],
    )


def apply_kernel(
    place_ref,
    group_ref,
    ahead2_ref,
    behind2_ref,
    ahead1_ref,
    behind1_ref,
    nodes_ref,
    vecs_ref,
    steps_ref,
    cot_ref,
    init_ref,
    recinit_ref,
    wrec_ref,
    state_ref,
    adjoint_ref,
):
    per_block = H // BLOCKS
    ahead3, behind3 = links(group_ref, wrec_ref)
    u_right, u_right_t = weights_of(wrec_ref)
    init = init_ref[...]
    rec = recinit_ref[...]
    write, terms, off = gates(
        [group_ref[0, ROW_PROJ + p : ROW_PROJ + p + 1] for p in range(3)], parts3(rec), init
    )
    state = (
        init
        + (terms[0] * rec[:, :H] + terms[1] * rec[:, H : 2 * H] + terms[2] * rec[:, 2 * H :])
        - write * init
        + off
    )
    costate = jnp.zeros((1, H), F32)

    levels = [
        ([a[0] for a in ahead3], [a[1] for a in ahead3], [b[0] for b in behind3], [b[2] for b in behind3])
    ]
    for ahead_ref, behind_ref in ((ahead2_ref, behind2_ref), (ahead1_ref, behind1_ref)):
        levels.append(
            (
                [ahead_ref[j, :H] for j in range(3)],
                [ahead_ref[j, H : H + 1] for j in range(3)],
                [behind_ref[j, :H] for j in range(3)],
                [behind_ref[j, H : H + 1] for j in range(3)],
            )
        )
    for level, (fm, fv, bm, bv) in enumerate(levels):
        own = place_ref[level]
        for j in range(3):
            moved = state + vec_mm(state, fm[j]) + fv[j]
            state = jnp.where(j < own, moved, state)
            i = 2 - j
            moved = costate + vec_mm_t(costate, bm[i]) + bv[i]
            costate = jnp.where(i >= own, moved, costate)

    states = {1: state}
    costates = {1: costate}
    for n in range(1, BLOCKS):
        states[2 * n] = states[n]
        states[2 * n + 1] = (
            states[n] + vec_mm(states[n], nodes_ref[2 * n]) + vecs_ref[2 * n : 2 * n + 1, :H]
        )
        costates[2 * n + 1] = costates[n]
        costates[2 * n] = (
            costates[n]
            + vec_mm_t(costates[n], nodes_ref[2 * n + 1])
            + vecs_ref[2 * n + 1 : 2 * n + 2, H:]
        )
    fwd = jnp.concatenate([states[BLOCKS + k] for k in range(BLOCKS)], axis=0)
    bwd = jnp.concatenate([costates[BLOCKS + k] for k in range(BLOCKS)], axis=0)
    for l in range(per_block):
        fwd = forward_step(fwd, steps_ref, l, u_right, per_block)
        state_ref.at[0][pl.ds(l, BLOCKS, stride=per_block), :] = fwd
        back = per_block - 1 - l
        out, bwd = backward_step(bwd, steps_ref, cot_ref, back, u_right_t, per_block)
        adjoint_ref.at[0][pl.ds(back, BLOCKS, stride=per_block), :] = out


def call(kernel, out_shape, flops, count, scalars=0):
    vmem = pl.BlockSpec(memory_space=pltpu.VMEM)
    smem = pl.BlockSpec(memory_space=pltpu.SMEM)
    return pl.pallas_call(
        kernel,
        out_shape=out_shape,
        in_specs=[smem] * scalars + [vmem] * (count - scalars),
        out_specs=tuple(vmem for _ in out_shape),
        compiler_params=pltpu.CompilerParams(vmem_limit_bytes=VMEM_LIMIT),
        cost_estimate=pl.CostEstimate(flops=flops, bytes_accessed=2**20, transcendentals=0),
    )


def group_lists(count):
    near = [list(range(s, s + 4)) for s in range(0, count, 4)]
    middle = [
        [16 * y + i, 16 * y + 4 + i, 16 * y + 11 - i, 16 * y + 15 - i]
        for y in range(count // 16)
        for i in range(4)
    ]
    far = [[16 * y + z for y in range(4)] for z in range(16)]
    return near, middle, far


def shape(*dims):
    return jax.ShapeDtypeStruct(dims, F32)


def per_device(
    inputs, trajectory, initial_state, cotangent, in_weight, recurrent_weight, gate_bias
):
    near, middle, far = group_lists(lax.axis_size("seq"))
    place = lax.axis_index("seq")
    places = jnp.stack([place // 16, place // 4 % 4, place % 4]).astype(jnp.int32)
    pack, nodes, vecs, steps, recinit = call(
        local_kernel,
        (
            shape(4, ROWS, H),
            shape(2 * BLOCKS, H, H),
            shape(2 * BLOCKS, 2 * H),
            shape(5, H, H),
            shape(1, 3 * H),
        ),
        2 * 10**9,
        7,
    )(
        inputs,
        trajectory,
        cotangent,
        initial_state,
        in_weight,
        recurrent_weight,
        gate_bias.reshape(1, -1),
    )
    merge = call(
        merge_kernel, (shape(4, ROWS, H), shape(3, H + 8, H), shape(3, H + 8, H)), 10**8, 2
    )

    def exchange(packed, groups):
        return lax.all_to_all(packed, "seq", 0, 0, axis_index_groups=groups)

    pack, ahead1, behind1 = merge(exchange(pack, near), recurrent_weight)
    pack, ahead2, behind2 = merge(exchange(pack, middle), recurrent_weight)
    group = exchange(pack, far)
    new_state, adjoint = call(apply_kernel, (shape(1, H, H), shape(1, H, H)), 10**8, 13, 1)(
        places,
        group,
        ahead2,
        behind2,
        ahead1,
        behind1,
        nodes,
        vecs,
        steps,
        cotangent,
        initial_state,
        recinit,
        recurrent_weight,
    )
    return new_state, adjoint


def solution(mesh):
    return jax.shard_map(
        per_device,
        mesh=mesh,
        in_specs=(
            P("dp", "seq", None),
            P("dp", "seq", None),
            P("dp", None),
            P("dp", "seq", None),
            P(),
            P(),
            P(),
        ),
        out_specs=(P("dp", "seq", None), P("dp", "seq", None)),
        check_vma=False,
    )
```

time: 519 us -> 88.8 us (0.17)
  the two profiles are of different devices: /device:TPU:504 before, /device:TPU:6 now
where the time goes in v1:
time: 88.8 us; the launch traced here: 88.2 us
  blocking collectives  45.5 us (51%)
  Pallas kernels  21.8 us (25%)
  local copies, waits for them, and re-layouts  8.93 us (10%)
  waiting for transfers between devices  6.78 us (8%)
  starting transfers between devices  4.47 us (5%)
    all_to_all x2, blocking collectives, exchange(): return lax.all_to_all(packed, 'seq', 0, 0, axis_index_groups=groups)  45.5 us
    pallas_call x1, Pallas kernels, per_device(): call(local_kernel, (shape(4, ROWS, H), shape(2 * BLOCKS, H, H), shape(2 *...  14.2 us
    unnamed x26, local copies, waits for them, and re-layouts  8.24 us
    all_to_all x1, waiting for transfers between devices, exchange(): return lax.all_to_all(packed, 'seq', 0, 0, axis_index_groups=groups)  6.78 us
    pallas_call x1, Pallas kernels, per_device(): call(apply_kernel, (shape(1, H, H), shape(1, H, H)), 10 ** 8, 13, 1)  5.41 us
    all_to_all x1, starting transfers between devices, exchange(): return lax.all_to_all(packed, 'seq', 0, 0, axis_index_groups=groups)  4.47 us
  transfers between devices with their start and end apart: 1, of which 1 were waited for; matrix products, arithmetic and copies ran while one was open for 0% of the time, Pallas kernels for 0%

profile of v1, /device:TPU:6, one launch (start us, length us, event | category | flops | bytes accessed | tf_op | source)
XLA Modules:
  0.0 88.2 jit_solution(8642817220588081473)
XLA Ops:
  0.6 0.7 reshape.7.bias_ref
  1.3 0.0 copy-start
  1.3 0.9 %copy-done = f32[128,384]{1,0:T(8,128)S(1)} copy-done((f32[128,384]{1,0:T(8,128)S(1)}, f32[128,384]{1,0:T(8,128)}, u32[]{:S(2)}) %copy-start) | copy-done | bytes 196632
  2.2 0.0 copy-start.4
  2.2 0.8 copy-done.4
  3.1 0.0 copy-start.8
  3.1 0.7 copy-done.8
  3.7 0.0 copy-start.10
  3.7 0.9 %copy-done.10 = f32[128,384]{1,0:T(8,128)S(1)} copy-done((f32[128,384]{1,0:T(8,128)S(1)}, f32[128,384]{1,0:T(8,128)}, u32[]{:S(2)}) %copy-start.10) | copy-done | bytes 196632
  4.7 0.0 copy-start.11
  4.7 0.8 copy-done.11
  5.5 0.0 copy-start.12
  5.5 0.8 copy-done.12
  6.3 0.0 copy-start.1
  6.3 14.2 %shard_map.86 = (f32[4,144,128]{2,1,0:T(8,128)S(1)}, f32[32,128,128]{2,1,0:T(8,128)S(1)}, f32[32,256]{1,0:T(8,128)S(1)}, f32[5,128,128]{2,1,0:T(8,128)S(1)}, f32[1,384]{1,0:T(1,128)S(1)}) custom-call(f32[1,128,128]{2,1,0:T(8,128)S(1)} %copy-done.11, f32[1,128,128]{2,1,0:T(8,128)S(1)} %copy-done.12, f32[1,128,128]{2,1,0:T(8,128)S(1)} %copy-done.4, ...), custom_call_target="tpu_custom_call" | custom-call | flops 2000000000 | bytes 1048576 | tf_op jit(solution)/shard_map/pallas_call | solution.py:405
  20.5 0.0 copy-start.6
  20.5 0.0 copy-start.9
  20.5 15.4 %all_to_all.15.group_ref = f32[4,144,128]{2,1,0:T(8,128)S(1)} all-to-all(f32[4,144,128]{2,1,0:T(8,128)S(1)} %get-tuple-element.13), channel_id=1, replica_groups={{0,1,2,3},{4,5,6,7},{8,9,10,11},{12,13,14,15},{16,17,18,19},{20,21,22,2..., dimensions={0} | all-to-all | bytes 589824 | tf_op jit(solution)/shard_map/all_to_all | solution.py:430
  35.9 0.0 copy-done.1
  35.9 0.7 shard_map.87
  36.7 0.0 copy-done.6
  36.7 30.1 %all_to_all.16.group_ref = f32[4,144,128]{2,1,0:T(8,128)S(1)} all-to-all(f32[4,144,128]{2,1,0:T(8,128)S(1)} %get-tuple-element.14), channel_id=1, replica_groups={{0,4,11,15},{1,5,10,14},{2,6,9,13},{3,7,8,12},{16,20,27,31},{17,21,26,3..., dimensions={0} | all-to-all | bytes 589824 | tf_op jit(solution)/shard_map/all_to_all | solution.py:430
  66.8 1.4 %shard_map.88 = (f32[4,144,128]{2,1,0:T(8,128)}, f32[3,136,128]{2,1,0:T(8,128)S(1)}, f32[3,136,128]{2,1,0:T(8,128)S(1)}) custom-call(f32[4,144,128]{2,1,0:T(8,128)S(1)} %all_to_all.16.group_ref, f32[128,384]{1,0:T(8,128)S(1)} %copy-done.1), custom_call_target="tpu_custom_call" | custom-call | flops 100000000 | bytes 1048576 | tf_op jit(solution)/shard_map/pallas_call | solution.py:433
  68.3 0.0 copy-start.2
  68.3 0.7 copy-done.2
  68.9 4.5 %all-to-all-start.2 = ((f32[4,144,128]{2,1,0:T(8,128)}), f32[4,144,128]{2,1,0:T(8,128)S(1)}, u32[]{:S(2)}, u32[]{:S(2)}) async-start(f32[4,144,128]{2,1,0:T(8,128)} %get-tuple-element.15), calls=%async_computation.2 | async-start | bytes 589824 | tf_op jit(solution)/shard_map/all_to_all | solution.py:430
  73.4 0.1 pad_add_fusion.place_ref
  73.5 6.8 %all-to-all-done.2.group_ref = f32[4,144,128]{2,1,0:T(8,128)S(1)} async-done(((f32[4,144,128]{2,1,0:T(8,128)}), f32[4,144,128]{2,1,0:T(8,128)S(1)}, u32[]{:S(2)}, u32[]{:S(2)}) %all-to-all-start.2) | async-done | bytes 294944 | tf_op jit(solution)/shard_map/all_to_all | solution.py:430
  80.3 0.0 copy-done.9
  80.3 0.0 copy-start.3
  80.3 0.9 %copy-done.3 = f32[3,136,128]{2,1,0:T(8,128)S(1)} copy-done((f32[3,136,128]{2,1,0:T(8,128)S(1)}, f32[3,136,128]{2,1,0:T(8,128)}, u32[]{:S(2)}) %copy-start.3) | copy-done | bytes 208920
  81.2 0.0 copy-start.5
  81.2 0.8 copy-done.5
  82.0 0.0 copy-start.7
  82.0 0.8 copy-done.7
  82.8 5.4 %shard_map.89 = (f32[1,128,128]{2,1,0:T(8,128)}, f32[1,128,128]{2,1,0:T(8,128)}) custom-call(s32[3]{0:T(128)S(1)} %pad_add_fusion.place_ref, f32[4,144,128]{2,1,0:T(8,128)S(1)} %all-to-all-done.2.group_ref, f32[3,136,128]{2,1,0:T(8,128)S(1)} %get-tuple-element.16.ahead2_ref, f32[3,136,128]{2,1,0:T(8,128)S(1)} %copy-done.3, ...), custom_call_target="tpu_custom_call" | custom-call | flops 100000000 | bytes 1048576 | tf_op jit(solution)/shard_map/pallas_call | solution.py:435
Async XLA Ops:
  1.3 0.9 %copy-start = (f32[128,384]{1,0:T(8,128)S(1)}, f32[128,384]{1,0:T(8,128)}, u32[]{:S(2)}) copy-start(f32[128,384]{1,0:T(8,128)} %wrec_ref.7) | copy-start | bytes 589828
  2.2 0.8 copy-start.4
  3.1 0.7 copy-start.8
  3.7 0.9 %copy-start.10 = (f32[128,384]{1,0:T(8,128)S(1)}, f32[128,384]{1,0:T(8,128)}, u32[]{:S(2)}) copy-start(f32[128,384]{1,0:T(8,128)} %win_ref.1) | copy-start | bytes 589828
  4.7 0.8 copy-start.11
  5.5 0.8 copy-start.12
  6.3 29.6 %copy-start.1 = (f32[128,384]{1,0:T(8,128)S(1)}, f32[128,384]{1,0:T(8,128)}, u32[]{:S(2)}) copy-start(f32[128,384]{1,0:T(8,128)} %wrec_ref.7) | copy-start | bytes 589828
  20.5 16.2 %copy-start.6 = (f32[32,256]{1,0:T(8,128)}, f32[32,256]{1,0:T(8,128)S(1)}, u32[]{:S(2)}) copy-start(f32[32,256]{1,0:T(8,128)S(1)} %get-tuple-element.21.vecs_ref) | copy-start | bytes 98308
  20.5 59.7 %copy-start.9 = (f32[1,128]{1,0:T(1,128)S(1)}, f32[1,128]{1,0:T(1,128)}, u32[]{:S(2)}) copy-start(f32[1,128]{1,0:T(1,128)} %init_ref.3) | copy-start | bytes 1540
  68.3 0.7 copy-start.2
  68.9 11.3 %all-to-all-start.2 = ((f32[4,144,128]{2,1,0:T(8,128)}), f32[4,144,128]{2,1,0:T(8,128)S(1)}, u32[]{:S(2)}, u32[]{:S(2)}) async-start(f32[4,144,128]{2,1,0:T(8,128)} %get-tuple-element.15), calls=%async_computation.2 | async-start | bytes 589824 | tf_op jit(solution)/shard_map/all_to_all | solution.py:430
  80.3 0.9 %copy-start.3 = (f32[3,136,128]{2,1,0:T(8,128)S(1)}, f32[3,136,128]{2,1,0:T(8,128)}, u32[]{:S(2)}) copy-start(f32[3,136,128]{2,1,0:T(8,128)} %copy-done.2) | copy-start | bytes 626692
  81.2 0.8 copy-start.5
  82.0 0.8 copy-start.7

commit v2 on v1

--- a/solution.py
+++ b/solution.py
@@ -15,7 +15,7 @@
 ROW_REC = 133
 ROW_LAST = 136
 ROWS = 144
-VMEM_LIMIT = 48 * 1024 * 1024
+VMEM_LIMIT = 24 * 1024 * 1024
 
 
 def split(x):
@@ -108,6 +108,16 @@
 
 
 def local_kernel(
+    x_hbm,
+    traj_hbm,
+    cot_hbm,
+    init_hbm,
+    win_hbm,
+    wrec_hbm,
+    bias_hbm,
+    pack_ref,
+    nodes_ref,
+    steps_hbm,
     x_ref,
     traj_ref,
     cot_ref,
@@ -115,23 +125,42 @@
     win_ref,
     wrec_ref,
     bias_ref,
-    pack_ref,
-    nodes_ref,
-    vecs_ref,
     steps_ref,
-    recinit_ref,
+    pairs_ref,
+    quads_ref,
+    sems,
 ):
+    copies = [
+        pltpu.make_async_copy(src, dst, sems.at[i])
+        for i, (src, dst) in enumerate(
+            (
+                (traj_hbm, traj_ref),
+                (wrec_hbm, wrec_ref),
+                (init_hbm, init_ref),
+                (x_hbm, x_ref),
+                (win_hbm, win_ref),
+                (bias_hbm, bias_ref),
+                (cot_hbm, cot_ref),
+            )
+        )
+    ]
+    for copy in copies:
+        copy.start()
+    for copy in copies[:3]:
+        copy.wait()
     traj = traj_ref[0]
-    proj = (
-        jnp.dot(x_ref[0], win_ref[...], precision=lax.Precision.HIGHEST, preferred_element_type=F32)
-        + bias_ref[...]
-    )
     rec_in = jnp.concatenate([traj, pad8(init_ref[...])], axis=0)
     rec_all = jnp.dot(
         rec_in, wrec_ref[...], precision=lax.Precision.HIGHEST, preferred_element_type=F32
     )
-    recinit_ref[...] = rec_all[H : H + 1]
+    rec_init = rec_all[H : H + 1]
     rec_rows = rec_all[:H]
+    for copy in copies[3:]:
+        copy.wait()
+    proj = (
+        jnp.dot(x_ref[0], win_ref[...], precision=lax.Precision.HIGHEST, preferred_element_type=F32)
+        + bias_ref[...].reshape(1, 3 * H)
+    )
     rec = pltpu.roll(rec_rows, 1, 0)
     prev = pltpu.roll(traj, 1, 0)
     write, terms, off = gates(parts3(proj), parts3(rec), prev)
@@ -141,46 +170,61 @@
     off = jnp.where(inner, off, 0.0)
     for p, rows in enumerate((*terms, write, off)):
         steps_ref[p] = rows
+    save = pltpu.make_async_copy(steps_ref, steps_hbm, sems.at[7])
+    save.start()
 
     ident = eye()
     per_block = H // BLOCKS
-
-    def one_block(k, carry):
-        base = pl.multiple_of(k * per_block, per_block)
-        rows = [steps_ref[p, pl.ds(base, per_block), :] for p in range(4)]
-        u = [wrec_ref[:, p * H : (p + 1) * H] for p in range(3)]
-        maps = []
-        for l in range(per_block):
-            row = [r[l : l + 1] for r in rows]
-            maps.append(leaf(u, row[3], row[:3], ident))
-        while len(maps) > 1:
-            maps = [
-                maps[i] + maps[i + 1] + mm(maps[i], maps[i + 1]) for i in range(0, len(maps), 2)
-            ]
-        nodes_ref[BLOCKS + k] = maps[0]
+    u_right, u_right_t = weights_of(wrec_ref)
+
+    def some_pairs(k, carry):
+        fwd, bwd = carry
+        base = pl.multiple_of(k * 16, 16)
+        for half in range(2):
+            rows = [steps_ref[p, pl.ds(base + 8 * half, 8), :] for p in range(4)]
+            u = [wrec_ref[:, p * H : (p + 1) * H] for p in range(3)]
+            for i in range(4):
+                maps = []
+                for l in (2 * i, 2 * i + 1):
+                    row = [r[l : l + 1] for r in rows]
+                    maps.append(leaf(u, row[3], row[:3], ident))
+                pairs_ref[8 * k + 4 * half + i] = maps[0] + maps[1] + mm(*maps)
+        fwd = forward_step(fwd, steps_ref, k, u_right, per_block)
+        _, bwd = backward_step(bwd, steps_ref, cot_ref, per_block - 1 - k, u_right_t, per_block)
+        return fwd, bwd
+
+    zero = jnp.zeros((BLOCKS, H), F32)
+    fwd, bwd = lax.fori_loop(0, 8, some_pairs, (zero, zero))
+    for k in range(BLOCKS):
+        nodes_ref[BLOCKS + k, H:] = two_rows(fwd[k : k + 1], bwd[k : k + 1])
+
+    def joined(ref, i):
+        early, late = ref[2 * i], ref[2 * i + 1]
+        return early + late + mm(early, late)
+
+    def some_quads(k, carry):
+        for i in range(8):
+            quads_ref[8 * k + i] = joined(pairs_ref, 8 * k + i)
         return carry
 
-    lax.fori_loop(0, BLOCKS, one_block, 0)
-
-    u_right, u_right_t = weights_of(wrec_ref)
-    fwd = jnp.zeros((BLOCKS, H), F32)
-    bwd = jnp.zeros((BLOCKS, H), F32)
-    for l in range(per_block):
-        fwd = forward_step(fwd, steps_ref, l, u_right, per_block)
-        _, bwd = backward_step(bwd, steps_ref, cot_ref, per_block - 1 - l, u_right_t, per_block)
-    vecs_ref[BLOCKS : 2 * BLOCKS, :H] = fwd
-    vecs_ref[BLOCKS : 2 * BLOCKS, H:] = bwd
+    lax.fori_loop(0, 4, some_quads, 0)
+
+    def some_blocks(k, carry):
+        for i in range(8):
+            nodes_ref[BLOCKS + 8 * k + i, :H] = joined(quads_ref, 8 * k + i)
+        return carry
+
+    lax.fori_loop(0, 2, some_blocks, 0)
 
     def node(n):
-        return nodes_ref[n], vecs_ref[n : n + 1, :H], vecs_ref[n : n + 1, H:]
+        return nodes_ref[n, :H], nodes_ref[n, H : H + 1], nodes_ref[n, H + 1 : H + 2]
 
     for n in range(BLOCKS - 1, 0, -1):
         m, v, c = compose(node(2 * n), node(2 * n + 1))
-        nodes_ref[n] = m
-        vecs_ref[n : n + 1, :H] = v
-        vecs_ref[n : n + 1, H:] = c
-    nodes_ref[0] = jnp.zeros((H, H), F32)
-    vecs_ref[0:1, :] = jnp.zeros((1, 2 * H), F32)
+        nodes_ref[n, :H] = m
+        nodes_ref[n, H:] = two_rows(v, c)
+    nodes_ref[0, :8] = jnp.concatenate([*parts3(rec_init), jnp.zeros((5, H), F32)], axis=0)
+    nodes_ref[0, 8:] = jnp.zeros((H, H), F32)
     m, v, c = node(1)
     rec_last = rec_rows[H - 1 : H]
     write_pack(
@@ -191,6 +235,11 @@
         + [rec_last[:, p * H : (p + 1) * H] for p in range(3)]
         + [traj[H - 1 : H]],
     )
+    save.wait()
+
+
+def two_rows(v, c):
+    return jnp.concatenate([v, c, jnp.zeros((6, H), F32)], axis=0)
 
 
 def write_pack(pack_ref, m, rows):
@@ -266,15 +315,15 @@
     return ahead, behind
 
 
-def merge_kernel(group_ref, wrec_ref, pack_ref, ahead_ref, behind_ref):
+def merge_kernel(group_ref, wrec_ref, pack_ref, links_ref):
     ahead, behind = links(group_ref, wrec_ref)
     for j in range(3):
         m, v = ahead[j]
-        ahead_ref[j, :H] = m
-        ahead_ref[j, H:] = pad8(v)
+        links_ref[j, :H] = m
+        links_ref[j, H:] = pad8(v)
         m, v, c = behind[j]
-        behind_ref[j, :H] = m
-        behind_ref[j, H:] = pad8(c)
+        links_ref[3 + j, :H] = m
+        links_ref[3 + j, H:] = pad8(c)
     start = (
         group_ref[0, :H],
         group_ref[0, ROW_B : ROW_B + 1],
@@ -292,33 +341,40 @@
 
 
 def apply_kernel(
-    place_ref,
     group_ref,
-    ahead2_ref,
-    behind2_ref,
-    ahead1_ref,
-    behind1_ref,
+    links2_ref,
+    links1_ref,
     nodes_ref,
-    vecs_ref,
+    steps_hbm,
+    cot_hbm,
+    init_hbm,
+    wrec_ref,
+    state_ref,
+    adjoint_ref,
     steps_ref,
     cot_ref,
     init_ref,
-    recinit_ref,
-    wrec_ref,
-    state_ref,
-    adjoint_ref,
+    sems,
 ):
+    copies = [
+        pltpu.make_async_copy(init_hbm, init_ref, sems.at[0]),
+        pltpu.make_async_copy(steps_hbm, steps_ref, sems.at[1]),
+        pltpu.make_async_copy(cot_hbm, cot_ref, sems.at[2]),
+    ]
+    for copy in copies:
+        copy.start()
     per_block = H // BLOCKS
     ahead3, behind3 = links(group_ref, wrec_ref)
     u_right, u_right_t = weights_of(wrec_ref)
+    copies[0].wait()
     init = init_ref[...]
-    rec = recinit_ref[...]
+    rec = [nodes_ref[0, p : p + 1] for p in range(3)]
     write, terms, off = gates(
-        [group_ref[0, ROW_PROJ + p : ROW_PROJ + p + 1] for p in range(3)], parts3(rec), init
+        [group_ref[0, ROW_PROJ + p : ROW_PROJ + p + 1] for p in range(3)], rec, init
     )
     state = (
         init
-        + (terms[0] * rec[:, :H] + terms[1] * rec[:, H : 2 * H] + terms[2] * rec[:, 2 * H :])
+        + (terms[0] * rec[0] + terms[1] * rec[1] + terms[2] * rec[2])
         - write * init
         + off
     )
@@ -327,17 +383,19 @@
     levels = [
         ([a[0] for a in ahead3], [a[1] for a in ahead3], [b[0] for b in behind3], [b[2] for b in behind3])
     ]
-    for ahead_ref, behind_ref in ((ahead2_ref, behind2_ref), (ahead1_ref, behind1_ref)):
+    for links_ref in (links2_ref, links1_ref):
         levels.append(
             (
-                [ahead_ref[j, :H] for j in range(3)],
-                [ahead_ref[j, H : H + 1] for j in range(3)],
-                [behind_ref[j, :H] for j in range(3)],
-                [behind_ref[j, H : H + 1] for j in range(3)],
+                [links_ref[j, :H] for j in range(3)],
+                [links_ref[j, H : H + 1] for j in range(3)],
+                [links_ref[3 + j, :H] for j in range(3)],
+                [links_ref[3 + j, H : H + 1] for j in range(3)],
             )
         )
+    place = lax.axis_index("seq")
+    places = (place // 16, place // 4 % 4, place % 4)
     for level, (fm, fv, bm, bv) in enumerate(levels):
-        own = place_ref[level]
+        own = places[level]
         for j in range(3):
             moved = state + vec_mm(state, fm[j]) + fv[j]
             state = jnp.where(j < own, moved, state)
@@ -350,16 +408,18 @@
     for n in range(1, BLOCKS):
         states[2 * n] = states[n]
         states[2 * n + 1] = (
-            states[n] + vec_mm(states[n], nodes_ref[2 * n]) + vecs_ref[2 * n : 2 * n + 1, :H]
+            states[n] + vec_mm(states[n], nodes_ref[2 * n, :H]) + nodes_ref[2 * n, H : H + 1]
         )
         costates[2 * n + 1] = costates[n]
         costates[2 * n] = (
             costates[n]
-            + vec_mm_t(costates[n], nodes_ref[2 * n + 1])
-            + vecs_ref[2 * n + 1 : 2 * n + 2, H:]
+            + vec_mm_t(costates[n], nodes_ref[2 * n + 1, :H])
+            + nodes_ref[2 * n + 1, H + 1 : H + 2]
         )
     fwd = jnp.concatenate([states[BLOCKS + k] for k in range(BLOCKS)], axis=0)
     bwd = jnp.concatenate([costates[BLOCKS + k] for k in range(BLOCKS)], axis=0)
+    for copy in copies[1:]:
+        copy.wait()
     for l in range(per_block):
         fwd = forward_step(fwd, steps_ref, l, u_right, per_block)
         state_ref.at[0][pl.ds(l, BLOCKS, stride=per_block), :] = fwd
@@ -368,17 +428,29 @@
         adjoint_ref.at[0][pl.ds(back, BLOCKS, stride=per_block), :] = out
 
 
-def call(kernel, out_shape, flops, count, scalars=0):
-    vmem = pl.BlockSpec(memory_space=pltpu.VMEM)
-    smem = pl.BlockSpec(memory_space=pltpu.SMEM)
-    return pl.pallas_call(
+def call(kernel, out_shape, flops, spaces, outs, scratch=()):
+    kinds = {"s": pltpu.SMEM, "v": pltpu.VMEM, "h": pltpu.HBM}
+    run = pl.pallas_call(
         kernel,
-        out_shape=out_shape,
-        in_specs=[smem] * scalars + [vmem] * (count - scalars),
-        out_specs=tuple(vmem for _ in out_shape),
+        out_shape=tuple(
+            pltpu.HBM(o.shape, o.dtype) if k == "h" else o for k, o in zip(outs, out_shape)
+        ),
+        in_specs=[pl.BlockSpec(memory_space=kinds[k]) for k in spaces],
+        out_specs=tuple(pl.BlockSpec(memory_space=kinds[k]) for k in outs),
+        scratch_shapes=list(scratch),
         compiler_params=pltpu.CompilerParams(vmem_limit_bytes=VMEM_LIMIT),
         cost_estimate=pl.CostEstimate(flops=flops, bytes_accessed=2**20, transcendentals=0),
     )
+
+    def placed(*args):
+        return run(
+            *(
+                pltpu.with_memory_space_constraint(a, pltpu.HBM) if k == "h" else a
+                for k, a in zip(spaces, args)
+            )
+        )
+
+    return placed
 
 
 def group_lists(count):
@@ -400,19 +472,29 @@
     inputs, trajectory, initial_state, cotangent, in_weight, recurrent_weight, gate_bias
 ):
     near, middle, far = group_lists(lax.axis_size("seq"))
-    place = lax.axis_index("seq")
-    places = jnp.stack([place // 16, place // 4 % 4, place % 4]).astype(jnp.int32)
-    pack, nodes, vecs, steps, recinit = call(
+    pack, nodes, steps = call(
         local_kernel,
         (
             shape(4, ROWS, H),
-            shape(2 * BLOCKS, H, H),
-            shape(2 * BLOCKS, 2 * H),
+            shape(2 * BLOCKS, H + 8, H),
             shape(5, H, H),
-            shape(1, 3 * H),
         ),
         2 * 10**9,
-        7,
+        "hhhhhhh",
+        "vvh",
+        [
+            pltpu.VMEM((1, H, H), F32),
+            pltpu.VMEM((1, H, H), F32),
+            pltpu.VMEM((1, H, H), F32),
+            pltpu.VMEM((1, H), F32),
+            pltpu.VMEM((H, 3 * H), F32),
+            pltpu.VMEM((H, 3 * H), F32),
+            pltpu.VMEM((3 * H,), F32),
+            pltpu.VMEM((5, H, H), F32),
+            pltpu.VMEM((64, H, H), F32),
+            pltpu.VMEM((32, H, H), F32),
+            pltpu.SemaphoreType.DMA((8,)),
+        ],
     )(
         inputs,
         trajectory,
@@ -420,31 +502,37 @@
         initial_state,
         in_weight,
         recurrent_weight,
-        gate_bias.reshape(1, -1),
+        gate_bias,
     )
     merge = call(
-        merge_kernel, (shape(4, ROWS, H), shape(3, H + 8, H), shape(3, H + 8, H)), 10**8, 2
+        merge_kernel, (shape(4, ROWS, H), shape(6, H + 8, H)), 10**8, "vv", "vv"
     )
 
     def exchange(packed, groups):
         return lax.all_to_all(packed, "seq", 0, 0, axis_index_groups=groups)
 
-    pack, ahead1, behind1 = merge(exchange(pack, near), recurrent_weight)
-    pack, ahead2, behind2 = merge(exchange(pack, middle), recurrent_weight)
+    pack, links1 = merge(exchange(pack, near), recurrent_weight)
+    pack, links2 = merge(exchange(pack, middle), recurrent_weight)
     group = exchange(pack, far)
-    new_state, adjoint = call(apply_kernel, (shape(1, H, H), shape(1, H, H)), 10**8, 13, 1)(
-        places,
+    new_state, adjoint = call(
+        apply_kernel,
+        (shape(1, H, H), shape(1, H, H)),
+        10**8, "vvvvhhhv",
+        "vv",
+        [
+            pltpu.VMEM((5, H, H), F32),
+            pltpu.VMEM((1, H, H), F32),
+            pltpu.VMEM((1, H), F32),
+            pltpu.SemaphoreType.DMA((3,)),
+        ],
+    )(
         group,
-        ahead2,
-        behind2,
-        ahead1,
-        behind1,
+        links2,
+        links1,
         nodes,
-        vecs,
         steps,
         cotangent,
         initial_state,
-        recinit,
         recurrent_weight,
     )
     return new_state, adjoint

time: 88.8 us -> 74.6 us (0.84)
  blocking collectives: 45.5 us -> 56.5 us
  local copies, waits for them, and re-layouts: 8.93 us -> 0.01 us
  waiting for transfers between devices: 6.78 us -> 0 us
  Pallas kernels: 21.8 us -> 17.2 us
  starting transfers between devices: 4.47 us -> 0 us
    all_to_all x2 -> x3, blocking collectives: 45.5 us -> 56.5 us  [exchange(): return lax.all_to_all(packed, 'seq', 0, 0, axis_index_groups=groups)]
    unnamed x26 -> x2, local copies, waits for them, and re-layouts: 8.24 us -> 0.01 us
    all_to_all x1 -> x0, waiting for transfers between devices: 6.78 us -> none  [exchange(): return lax.all_to_all(packed, 'seq', 0, 0, axis_index_groups=groups)]
    pallas_call x4, Pallas kernels: 21.8 us -> 17.2 us  [placed(): run(*(pltpu.with_memory_space_constraint(a, pltpu.HBM) if k == 'h' else a...]
    all_to_all x1 -> x0, starting transfers between devices: 4.47 us -> none  [exchange(): return lax.all_to_all(packed, 'seq', 0, 0, axis_index_groups=groups)]
  transfers between devices with their start and end apart: 1 -> 0, of which waited for: 1 -> 0; matrix products, arithmetic and copies ran while one was open for 0% -> 0% of each run, Pallas kernels for 0% -> 0%
where the time goes in v2:
time: 74.6 us; the launch traced here: 74.4 us
  blocking collectives  56.5 us (76%)
  Pallas kernels  17.2 us (23%)
    all_to_all x3, blocking collectives, exchange(): return lax.all_to_all(packed, 'seq', 0, 0, axis_index_groups=groups)  56.5 us
    pallas_call x4, Pallas kernels, placed(): run(*(pltpu.with_memory_space_constraint(a, pltpu.HBM) if k == 'h' else a...  17.2 us

profile of v2, /device:TPU:6, one launch (start us, length us, event | category | flops | bytes accessed | tf_op | source)
XLA Modules:
  0.0 74.4 jit_solution(7488051017377506029)
XLA Ops:
  0.6 0.0 copy-start
  0.6 10.4 %shard_map.86 = (f32[4,144,128]{2,1,0:T(8,128)S(1)}, f32[32,136,128]{2,1,0:T(8,128)S(1)}, f32[5,128,128]{2,1,0:T(8,128)}) custom-call(f32[1,128,128]{2,1,0:T(8,128)} %x_hbm.1, f32[1,128,128]{2,1,0:T(8,128)} %traj_hbm.1, f32[1,128,128]{2,1,0:T(8,128)} %cot_hbm.3, f32[1,128]{1,0:T(1,128)} %init_hbm.3, f32[128,384]{1,0:T(8,128)} %win_hbm.1, ...), custom_call_target="tpu_custom_call" | custom-call | flops 2000000000 | bytes 1048576 | tf_op jit(solution)/shard_map/pallas_call | solution.py:446
  11.0 15.3 %all_to_all.15.group_ref = f32[4,144,128]{2,1,0:T(8,128)S(1)} all-to-all(f32[4,144,128]{2,1,0:T(8,128)S(1)} %get-tuple-element.9), channel_id=1, replica_groups={{0,1,2,3},{4,5,6,7},{8,9,10,11},{12,13,14,15},{16,17,18,19},{20,21,22,2..., dimensions={0} | all-to-all | bytes 589824 | tf_op jit(solution)/shard_map/all_to_all | solution.py:512
  26.3 0.0 copy-done
  26.3 0.7 shard_map.87
  27.0 30.1 %all_to_all.16.group_ref = f32[4,144,128]{2,1,0:T(8,128)S(1)} all-to-all(f32[4,144,128]{2,1,0:T(8,128)S(1)} %get-tuple-element.10), channel_id=1, replica_groups={{0,4,11,15},{1,5,10,14},{2,6,9,13},{3,7,8,12},{16,20,27,31},{17,21,26,3..., dimensions={0} | all-to-all | bytes 589824 | tf_op jit(solution)/shard_map/all_to_all | solution.py:512
  57.2 0.7 shard_map.88
  57.9 11.1 %all_to_all.17.group_ref = f32[4,144,128]{2,1,0:T(8,128)S(1)} all-to-all(f32[4,144,128]{2,1,0:T(8,128)S(1)} %get-tuple-element.11), channel_id=1, replica_groups={{0,16,32,48},{1,17,33,49},{2,18,34,50},{3,19,35,51},{4,20,36,52},{5,21,..., dimensions={0} | all-to-all | bytes 589824 | tf_op jit(solution)/shard_map/all_to_all | solution.py:512
  69.0 5.4 %shard_map.89 = (f32[1,128,128]{2,1,0:T(8,128)}, f32[1,128,128]{2,1,0:T(8,128)}) custom-call(f32[4,144,128]{2,1,0:T(8,128)S(1)} %all_to_all.17.group_ref, f32[6,136,128]{2,1,0:T(8,128)S(1)} %get-tuple-element.12.links2_ref, f32[6,136,128]{2,1,0:T(8,128)S(1)} %get-tuple-element.13.links1_ref, f32[32,136,128]{2,1,0:T(8,128)S(1)} %get-tuple-element.14.nodes_ref, ...), custom_call_target="tpu_custom_call" | custom-call | flops 100000000 | bytes 1048576 | tf_op jit(solution)/shard_map/pallas_call | solution.py:446
Async XLA Ops:
  0.6 25.7 %copy-start = (f32[128,384]{1,0:T(8,128)S(1)}, f32[128,384]{1,0:T(8,128)}, u32[]{:S(2)}) copy-start(f32[128,384]{1,0:T(8,128)} %wrec_ref.5) | copy-start | bytes 589828

commit v3 on v2

--- a/solution.py
+++ b/solution.py
@@ -32,13 +32,6 @@
     return jnp.concatenate([row, row], axis=0)
 
 
-def right_t(x):
-    hi, lo = split(x)
-    return jnp.concatenate(
-        [jnp.concatenate([hi, hi], axis=1), jnp.concatenate([lo, lo], axis=1)], axis=0
-    )
-
-
 def both_halves(out):
     half = out.shape[1] // 2
     return out[:, :half] + out[:, half:]
@@ -48,24 +41,32 @@
     return both_halves(jnp.dot(left(a), right(b), preferred_element_type=F32))
 
 
-def mm_t(a, b):
-    return both_halves(
-        lax.dot_general(
-            left(a), right_t(b), (((1,), (1,)), ((), ())), preferred_element_type=F32
-        )
-    )
-
-
 def pad8(row):
     return jnp.broadcast_to(row, (8, H))
 
 
+def halves(x):
+    return jnp.concatenate(split(x), axis=1)
+
+
+def stacked(x):
+    return jnp.concatenate(split(x), axis=0)
+
+
+def few_rows(x, weights):
+    out = jnp.dot(stacked(x), weights, preferred_element_type=F32)
+    return both_halves(out[: x.shape[0]] + out[x.shape[0] :])
+
+
 def vec_mm(row, b):
-    return mm(pad8(row), b)[:1]
+    return few_rows(pad8(row), halves(b))[:1]
 
 
 def vec_mm_t(row, b):
-    return mm_t(pad8(row), b)[:1]
+    out = lax.dot_general(
+        stacked(pad8(row)), stacked(b), (((1,), (1,)), ((), ())), preferred_element_type=F32
+    )
+    return both_halves(out[:8] + out[8:])[:1]
 
 
 def eye():
@@ -175,7 +176,7 @@
 
     ident = eye()
     per_block = H // BLOCKS
-    u_right, u_right_t = weights_of(wrec_ref)
+    u_side, u_back = weights_of(wrec_ref)
 
     def some_pairs(k, carry):
         fwd, bwd = carry
@@ -189,12 +190,12 @@
                     row = [r[l : l + 1] for r in rows]
                     maps.append(leaf(u, row[3], row[:3], ident))
                 pairs_ref[8 * k + 4 * half + i] = maps[0] + maps[1] + mm(*maps)
-        fwd = forward_step(fwd, steps_ref, k, u_right, per_block)
-        _, bwd = backward_step(bwd, steps_ref, cot_ref, per_block - 1 - k, u_right_t, per_block)
+        fwd = forward_step(fwd, steps_ref, k, u_side, per_block)
+        _, bwd = backward_step(bwd, steps_ref, cot_ref, per_block - 1 - k, u_back, per_block)
         return fwd, bwd
 
     zero = jnp.zeros((BLOCKS, H), F32)
-    fwd, bwd = lax.fori_loop(0, 8, some_pairs, (zero, zero))
+    fwd, bwd = lax.fori_loop(0, 8, some_pairs, (zero, zero), unroll=8)
     for k in range(BLOCKS):
         nodes_ref[BLOCKS + k, H:] = two_rows(fwd[k : k + 1], bwd[k : k + 1])
 
@@ -207,14 +208,14 @@
             quads_ref[8 * k + i] = joined(pairs_ref, 8 * k + i)
         return carry
 
-    lax.fori_loop(0, 4, some_quads, 0)
+    lax.fori_loop(0, 4, some_quads, 0, unroll=4)
 
     def some_blocks(k, carry):
         for i in range(8):
             nodes_ref[BLOCKS + 8 * k + i, :H] = joined(quads_ref, 8 * k + i)
         return carry
 
-    lax.fori_loop(0, 2, some_blocks, 0)
+    lax.fori_loop(0, 2, some_blocks, 0, unroll=2)
 
     def node(n):
         return nodes_ref[n, :H], nodes_ref[n, H : H + 1], nodes_ref[n, H + 1 : H + 2]
@@ -251,29 +252,25 @@
 
 def weights_of(wrec_ref):
     u = wrec_ref[...]
-    return right(u), right_t(u)
+    return halves(u), halves(u.T)
 
 
 def every(ref, l, per_block):
     return ref[pl.ds(l, BLOCKS, stride=per_block), :]
 
 
-def forward_step(h, steps_ref, l, u_right, per_block):
+def forward_step(h, steps_ref, l, u_side, per_block):
     term = [every(steps_ref.at[p], l, per_block) for p in range(5)]
-    mapped = parts3(both_halves(jnp.dot(left(h), u_right, preferred_element_type=F32)))
+    mapped = parts3(few_rows(h, u_side))
     moved = term[0] * mapped[0] + term[1] * mapped[1] + term[2] * mapped[2]
     return h + (moved - term[3] * h) + term[4]
 
 
-def backward_step(carried, steps_ref, cot_ref, l, u_right_t, per_block):
+def backward_step(carried, steps_ref, cot_ref, l, u_back, per_block):
     term = [every(steps_ref.at[p], l, per_block) for p in range(4)]
     costate = carried + every(cot_ref.at[0], l, per_block)
     scaled = jnp.concatenate([term[p] * costate for p in range(3)], axis=1)
-    back = both_halves(
-        lax.dot_general(
-            left(scaled), u_right_t, (((1,), (1,)), ((), ())), preferred_element_type=F32
-        )
-    )
+    back = few_rows(scaled, u_back)
     return costate, costate + (back - term[3] * costate)
 
 
@@ -340,32 +337,138 @@
     )
 
 
+def places():
+    place = lax.axis_index("seq")
+    return place // 16, place // 4 % 4, place % 4
+
+
+def forward_join(early, late):
+    prod = mm(jnp.concatenate([early[0], pad8(early[1])], axis=0), late[0])
+    return early[0] + late[0] + prod[:H], early[1] + late[1] + prod[H : H + 1]
+
+
+def adjoint_join(early, late):
+    return (
+        early[0] + late[0] + mm(early[0], late[0]),
+        early[1] + late[1] + vec_mm_t(late[1], early[0]),
+    )
+
+
+def paths_to(own, links_ref):
+    ahead = [(links_ref[j, :H], links_ref[j, H : H + 1]) for j in range(3)]
+    behind = [(links_ref[3 + j, :H], links_ref[3 + j, H : H + 1]) for j in range(3)]
+    keep = lambda on, new, old: tuple(jnp.where(on, n, o) for n, o in zip(new, old))
+    none = (jnp.zeros((H, H), F32), jnp.zeros((1, H), F32))
+    to = keep(own > 0, ahead[0], none)
+    back = keep(own < 3, behind[2], none)
+    for j in (1, 2):
+        to = keep(own > j, forward_join(to, ahead[j]), to)
+        back = keep(own < 3 - j, adjoint_join(behind[2 - j], back), back)
+    return to, back
+
+
+def reach_kernel(
+    nodes_ref,
+    links1_ref,
+    links2_ref,
+    wrec_ref,
+    maps_hbm,
+    vecs_hbm,
+    u_hbm,
+    ut_hbm,
+    maps_ref,
+    vecs_ref,
+    u_ref,
+    ut_ref,
+    sems,
+):
+    _, middle, near = places()
+    to1, back1 = paths_to(near, links1_ref)
+    to2, back2 = paths_to(middle, links2_ref)
+    none = (jnp.zeros((H, H), F32), jnp.zeros((1, H), F32))
+
+    def put(slot, found, flip):
+        m, v = found or none
+        maps_ref[slot] = halves(m.T if flip else m)
+        vecs_ref[slot : slot + 1] = v
+
+    put(2 * BLOCKS, forward_join(to2, to1), False)
+    put(2 * BLOCKS + 1, adjoint_join(back1, back2), True)
+    vecs_ref[2 * BLOCKS + 2 :] = jnp.zeros((6, H), F32)
+
+    def node(n, row):
+        return nodes_ref[n, :H], nodes_ref[n, H + row : H + row + 1]
+
+    before, after = {1: None}, {1: None}
+    for n in range(1, BLOCKS):
+        before[2 * n] = before[n]
+        first = node(2 * n, 0)
+        before[2 * n + 1] = first if before[n] is None else forward_join(before[n], first)
+        after[2 * n + 1] = after[n]
+        last = node(2 * n + 1, 1)
+        after[2 * n] = last if after[n] is None else adjoint_join(last, after[n])
+    for k in range(BLOCKS):
+        put(k, before[BLOCKS + k], False)
+        put(BLOCKS + k, after[BLOCKS + k], True)
+    u = wrec_ref[...]
+    u_ref[...] = halves(u)
+    ut_ref[...] = halves(u.T)
+    copies = [
+        pltpu.make_async_copy(src, dst, sems.at[i])
+        for i, (src, dst) in enumerate(
+            ((maps_ref, maps_hbm), (vecs_ref, vecs_hbm), (u_ref, u_hbm), (ut_ref, ut_hbm))
+        )
+    ]
+    for copy in copies:
+        copy.start()
+    for copy in copies:
+        copy.wait()
+
+
+def moved_by(vector, weights):
+    return few_rows(pad8(vector), weights)[:1]
+
+
 def apply_kernel(
     group_ref,
-    links2_ref,
-    links1_ref,
     nodes_ref,
+    wrec_ref,
+    maps_hbm,
+    vecs_hbm,
+    u_hbm,
+    ut_hbm,
     steps_hbm,
     cot_hbm,
     init_hbm,
-    wrec_ref,
     state_ref,
     adjoint_ref,
+    maps_ref,
+    vecs_ref,
+    u_ref,
+    ut_ref,
     steps_ref,
     cot_ref,
     init_ref,
     sems,
 ):
     copies = [
-        pltpu.make_async_copy(init_hbm, init_ref, sems.at[0]),
-        pltpu.make_async_copy(steps_hbm, steps_ref, sems.at[1]),
-        pltpu.make_async_copy(cot_hbm, cot_ref, sems.at[2]),
+        pltpu.make_async_copy(src, dst, sems.at[i])
+        for i, (src, dst) in enumerate(
+            (
+                (init_hbm, init_ref),
+                (maps_hbm, maps_ref),
+                (vecs_hbm, vecs_ref),
+                (u_hbm, u_ref),
+                (ut_hbm, ut_ref),
+                (steps_hbm, steps_ref),
+                (cot_hbm, cot_ref),
+            )
+        )
     ]
     for copy in copies:
         copy.start()
     per_block = H // BLOCKS
-    ahead3, behind3 = links(group_ref, wrec_ref)
-    u_right, u_right_t = weights_of(wrec_ref)
+    ahead, behind = links(group_ref, wrec_ref)
     copies[0].wait()
     init = init_ref[...]
     rec = [nodes_ref[0, p : p + 1] for p in range(3)]
@@ -379,52 +482,28 @@
         + off
     )
     costate = jnp.zeros((1, H), F32)
-
-    levels = [
-        ([a[0] for a in ahead3], [a[1] for a in ahead3], [b[0] for b in behind3], [b[2] for b in behind3])
-    ]
-    for links_ref in (links2_ref, links1_ref):
-        levels.append(
-            (
-                [links_ref[j, :H] for j in range(3)],
-                [links_ref[j, H : H + 1] for j in range(3)],
-                [links_ref[3 + j, :H] for j in range(3)],
-                [links_ref[3 + j, H : H + 1] for j in range(3)],
-            )
-        )
-    place = lax.axis_index("seq")
-    places = (place // 16, place // 4 % 4, place % 4)
-    for level, (fm, fv, bm, bv) in enumerate(levels):
-        own = places[level]
-        for j in range(3):
-            moved = state + vec_mm(state, fm[j]) + fv[j]
-            state = jnp.where(j < own, moved, state)
-            i = 2 - j
-            moved = costate + vec_mm_t(costate, bm[i]) + bv[i]
-            costate = jnp.where(i >= own, moved, costate)
-
-    states = {1: state}
-    costates = {1: costate}
-    for n in range(1, BLOCKS):
-        states[2 * n] = states[n]
-        states[2 * n + 1] = (
-            states[n] + vec_mm(states[n], nodes_ref[2 * n, :H]) + nodes_ref[2 * n, H : H + 1]
-        )
-        costates[2 * n + 1] = costates[n]
-        costates[2 * n] = (
-            costates[n]
-            + vec_mm_t(costates[n], nodes_ref[2 * n + 1, :H])
-            + nodes_ref[2 * n + 1, H + 1 : H + 2]
-        )
-    fwd = jnp.concatenate([states[BLOCKS + k] for k in range(BLOCKS)], axis=0)
-    bwd = jnp.concatenate([costates[BLOCKS + k] for k in range(BLOCKS)], axis=0)
+    own = places()[0]
+    for j in range(3):
+        moved = state + vec_mm(state, ahead[j][0]) + ahead[j][1]
+        state = jnp.where(j < own, moved, state)
+        i = 2 - j
+        moved = costate + vec_mm_t(costate, behind[i][0]) + behind[i][2]
+        costate = jnp.where(i >= own, moved, costate)
     for copy in copies[1:]:
         copy.wait()
+    at = 2 * BLOCKS
+    state = state + moved_by(state, maps_ref[at]) + vecs_ref[at : at + 1]
+    costate = costate + moved_by(costate, maps_ref[at + 1]) + vecs_ref[at + 1 : at + 2]
+    fwd = jnp.concatenate([moved_by(state, maps_ref[k]) for k in range(BLOCKS)], axis=0)
+    fwd = state + fwd + vecs_ref[:BLOCKS]
+    bwd = jnp.concatenate([moved_by(costate, maps_ref[BLOCKS + k]) for k in range(BLOCKS)], axis=0)
+    bwd = costate + bwd + vecs_ref[BLOCKS : 2 * BLOCKS]
+    u_side, u_back = u_ref[...], ut_ref[...]
     for l in range(per_block):
-        fwd = forward_step(fwd, steps_ref, l, u_right, per_block)
+        fwd = forward_step(fwd, steps_ref, l, u_side, per_block)
         state_ref.at[0][pl.ds(l, BLOCKS, stride=per_block), :] = fwd
         back = per_block - 1 - l
-        out, bwd = backward_step(bwd, steps_ref, cot_ref, back, u_right_t, per_block)
+        out, bwd = backward_step(bwd, steps_ref, cot_ref, back, u_back, per_block)
         adjoint_ref.at[0][pl.ds(back, BLOCKS, stride=per_block), :] = out
 
 
@@ -514,27 +593,36 @@
     pack, links1 = merge(exchange(pack, near), recurrent_weight)
     pack, links2 = merge(exchange(pack, middle), recurrent_weight)
     group = exchange(pack, far)
+    found = (
+        (2 * BLOCKS + 2, H, 2 * H),
+        (2 * BLOCKS + 8, H),
+        (H, 6 * H),
+        (3 * H, 2 * H),
+    )
+    kinds = (BF16, F32, BF16, BF16)
+    buffers = [pltpu.VMEM(dims, kind) for dims, kind in zip(found, kinds)]
+    reached = call(
+        reach_kernel,
+        tuple(jax.ShapeDtypeStruct(dims, kind) for dims, kind in zip(found, kinds)),
+        5 * 10**8,
+        "vvvv",
+        "hhhh",
+        buffers + [pltpu.SemaphoreType.DMA((4,))],
+    )(nodes, links1, links2, recurrent_weight)
     new_state, adjoint = call(
         apply_kernel,
         (shape(1, H, H), shape(1, H, H)),
-        10**8, "vvvvhhhv",
+        10**8,
+        "vvvhhhhhhh",
         "vv",
-        [
+        buffers
+        + [
             pltpu.VMEM((5, H, H), F32),
             pltpu.VMEM((1, H, H), F32),
             pltpu.VMEM((1, H), F32),
-            pltpu.SemaphoreType.DMA((3,)),
+            pltpu.SemaphoreType.DMA((7,)),
         ],
-    )(
-        group,
-        links2,
-        links1,
-        nodes,
-        steps,
-        cotangent,
-        initial_state,
-        recurrent_weight,
-    )
+    )(group, nodes, recurrent_weight, *reached, steps, cotangent, initial_state)
     return new_state, adjoint
 
 

time: 74.6 us -> 71.8 us (0.962)
  blocking collectives: 56.5 us -> 45.4 us
  starting transfers between devices: 0 us -> 4.46 us
  waiting for transfers between devices: 0 us -> 3.75 us
  Pallas kernels: 17.2 us -> 16.4 us
    all_to_all x3 -> x2, blocking collectives: 56.5 us -> 45.4 us  [exchange(): return lax.all_to_all(packed, 'seq', 0, 0, axis_index_groups=groups)]
    all_to_all x0 -> x1, starting transfers between devices: none -> 4.46 us  [exchange(): return lax.all_to_all(packed, 'seq', 0, 0, axis_index_groups=groups)]
    all_to_all x0 -> x1, waiting for transfers between devices: none -> 3.75 us  [exchange(): return lax.all_to_all(packed, 'seq', 0, 0, axis_index_groups=groups)]
    pallas_call x4 -> x5, Pallas kernels: 17.2 us -> 16.4 us  [placed(): run(*(pltpu.with_memory_space_constraint(a, pltpu.HBM) if k == 'h' else a...]
  transfers between devices with their start and end apart: 0 -> 1, of which waited for: 0 -> 1; matrix products, arithmetic and copies ran while one was open for 0% -> 0% of each run, Pallas kernels for 0% -> 4%
where the time goes in v3:
time: 71.8 us; the launch traced here: 71.5 us
  blocking collectives  45.4 us (63%)
  Pallas kernels  16.4 us (23%)
  starting transfers between devices  4.46 us (6%)
  waiting for transfers between devices  3.75 us (5%)
    all_to_all x2, blocking collectives, exchange(): return lax.all_to_all(packed, 'seq', 0, 0, axis_index_groups=groups)  45.4 us
    pallas_call x5, Pallas kernels, placed(): run(*(pltpu.with_memory_space_constraint(a, pltpu.HBM) if k == 'h' else a...  16.4 us
    all_to_all x1, starting transfers between devices, exchange(): return lax.all_to_all(packed, 'seq', 0, 0, axis_index_groups=groups)  4.46 us
    all_to_all x1, waiting for transfers between devices, exchange(): return lax.all_to_all(packed, 'seq', 0, 0, axis_index_groups=groups)  3.75 us
  transfers between devices with their start and end apart: 1, of which 1 were waited for; matrix products, arithmetic and copies ran while one was open for 0% of the time, Pallas kernels for 4%

profile of v3, /device:TPU:6, one launch (start us, length us, event | category | flops | bytes accessed | tf_op | source)
XLA Modules:
  0.0 71.5 jit_solution(5787559096531478603)
XLA Ops:
  0.6 0.0 copy-start
  0.6 7.7 %shard_map.86 = (f32[4,144,128]{2,1,0:T(8,128)S(1)}, f32[32,136,128]{2,1,0:T(8,128)S(1)}, f32[5,128,128]{2,1,0:T(8,128)}) custom-call(f32[1,128,128]{2,1,0:T(8,128)} %x_hbm.1, f32[1,128,128]{2,1,0:T(8,128)} %traj_hbm.1, f32[1,128,128]{2,1,0:T(8,128)} %cot_hbm.3, f32[1,128]{1,0:T(1,128)} %init_hbm.3, f32[128,384]{1,0:T(8,128)} %win_hbm.1, ...), custom_call_target="tpu_custom_call" | custom-call | flops 2000000000 | bytes 1048576 | tf_op jit(solution)/shard_map/pallas_call | solution.py:525
  8.4 15.3 %all_to_all.15.group_ref = f32[4,144,128]{2,1,0:T(8,128)S(1)} all-to-all(f32[4,144,128]{2,1,0:T(8,128)S(1)} %get-tuple-element.13), channel_id=1, replica_groups={{0,1,2,3},{4,5,6,7},{8,9,10,11},{12,13,14,15},{16,17,18,19},{20,21,22,2..., dimensions={0} | all-to-all | bytes 589824 | tf_op jit(solution)/shard_map/all_to_all | solution.py:591
  23.7 0.0 copy-done
  23.7 0.7 shard_map.87
  24.4 30.1 %all_to_all.16.group_ref = f32[4,144,128]{2,1,0:T(8,128)S(1)} all-to-all(f32[4,144,128]{2,1,0:T(8,128)S(1)} %get-tuple-element.14), channel_id=1, replica_groups={{0,4,11,15},{1,5,10,14},{2,6,9,13},{3,7,8,12},{16,20,27,31},{17,21,26,3..., dimensions={0} | all-to-all | bytes 589824 | tf_op jit(solution)/shard_map/all_to_all | solution.py:591
  54.5 0.7 shard_map.88
  55.2 0.0 copy-start.1
  55.2 0.7 copy-done.1
  55.9 4.5 %all-to-all-start.2 = ((f32[4,144,128]{2,1,0:T(8,128)}), f32[4,144,128]{2,1,0:T(8,128)S(1)}, u32[]{:S(2)}, u32[]{:S(2)}) async-start(f32[4,144,128]{2,1,0:T(8,128)} %copy-done.1), calls=%async_computation.2 | async-start | bytes 589824 | tf_op jit(solution)/shard_map/all_to_all | solution.py:591
  60.4 3.1 %shard_map.89 = (bf16[34,128,256]{2,1,0:T(8,128)(2,1)}, f32[40,128]{1,0:T(8,128)}, bf16[128,768]{1,0:T(8,128)(2,1)}, bf16[384,256]{1,0:T(8,128)(2,1)}) custom-call(f32[32,136,128]{2,1,0:T(8,128)S(1)} %get-tuple-element.16.nodes_ref, f32[6,136,128]{2,1,0:T(8,128)S(1)} %get-tuple-element.17.links1_ref, f32[6,136,128]{2,1,0:T(8,128)S(1)} %get-tuple-element.18.links2_ref, ...), custom_call_target="tpu_custom_call" | custom-call | flops 500000000 | bytes 1048576 | tf_op jit(solution)/shard_map/pallas_call | solution.py:525
  63.5 3.7 %all-to-all-done.2.group_ref = f32[4,144,128]{2,1,0:T(8,128)S(1)} async-done(((f32[4,144,128]{2,1,0:T(8,128)}), f32[4,144,128]{2,1,0:T(8,128)S(1)}, u32[]{:S(2)}, u32[]{:S(2)}) %all-to-all-start.2) | async-done | bytes 294944 | tf_op jit(solution)/shard_map/all_to_all | solution.py:591
  67.2 4.2 %shard_map.90 = (f32[1,128,128]{2,1,0:T(8,128)}, f32[1,128,128]{2,1,0:T(8,128)}) custom-call(f32[4,144,128]{2,1,0:T(8,128)S(1)} %all-to-all-done.2.group_ref, f32[32,136,128]{2,1,0:T(8,128)S(1)} %get-tuple-element.16.nodes_ref, f32[128,384]{1,0:T(8,128)S(1)} %copy-done, bf16[34,128,256]{2,1,0:T(8,128)(2,1)} %get-tuple-element.19.maps_hbm, ...), custom_call_target="tpu_custom_call" | custom-call | flops 100000000 | bytes 1048576 | tf_op jit(solution)/shard_map/pallas_call | solution.py:525
Async XLA Ops:
  0.6 23.0 %copy-start = (f32[128,384]{1,0:T(8,128)S(1)}, f32[128,384]{1,0:T(8,128)}, u32[]{:S(2)}) copy-start(f32[128,384]{1,0:T(8,128)} %wrec_ref.7) | copy-start | bytes 589828
  55.2 0.7 %copy-start.1 = (f32[4,144,128]{2,1,0:T(8,128)}, f32[4,144,128]{2,1,0:T(8,128)S(1)}, u32[]{:S(2)}) copy-start(f32[4,144,128]{2,1,0:T(8,128)S(1)} %get-tuple-element.15) | copy-start | bytes 884740
  55.9 11.3 %all-to-all-start.2 = ((f32[4,144,128]{2,1,0:T(8,128)}), f32[4,144,128]{2,1,0:T(8,128)S(1)}, u32[]{:S(2)}, u32[]{:S(2)}) async-start(f32[4,144,128]{2,1,0:T(8,128)} %copy-done.1), calls=%async_computation.2 | async-start | bytes 589824 | tf_op jit(solution)/shard_map/all_to_all | solution.py:591

commit v4 on v3

--- a/solution.py
+++ b/solution.py
@@ -1,3 +1,5 @@
+import functools
+
 import jax
 import jax.numpy as jnp
 from jax import lax
@@ -339,7 +341,7 @@
 
 def places():
     place = lax.axis_index("seq")
-    return place // 16, place // 4 % 4, place % 4
+    return place // 16, place % 4
 
 
 def forward_join(early, late):
@@ -367,10 +369,47 @@
     return to, back
 
 
+def pair_kernel(own_ref, other_ref, wrec_ref, pack_ref, path_ref, *, bit):
+    second = lax.axis_index("seq") // bit % 2 == 1
+    own, other = own_ref[0], other_ref[0]
+    early = jnp.where(second, other, own)
+    late = jnp.where(second, own, other)
+    u = [wrec_ref[:, p * H : (p + 1) * H] for p in range(3)]
+    write, terms, off = gates(
+        [late[ROW_PROJ + p : ROW_PROJ + p + 1] for p in range(3)],
+        [early[ROW_REC + p : ROW_REC + p + 1] for p in range(3)],
+        early[ROW_LAST : ROW_LAST + 1],
+    )
+    first = leaf(u, write, terms, eye())
+    early_v, early_c = early[ROW_B : ROW_B + 1], early[ROW_C : ROW_C + 1]
+    late_v, late_c = late[ROW_B : ROW_B + 1], late[ROW_C : ROW_C + 1]
+    ahead = forward_join((early[:H], early_v), (first, off))
+    prod = mm(jnp.concatenate([first, pad8(off)], axis=0), late[:H])
+    behind = (
+        first + late[:H] + prod[:H],
+        off + prod[H : H + 1] + late_v,
+        late_c + vec_mm_t(late_c, first),
+    )
+    path_ref[0, :H] = jnp.where(second, ahead[0], 0.0)
+    path_ref[0, H:] = pad8(jnp.where(second, ahead[1], 0.0))
+    path_ref[1, :H] = jnp.where(second, 0.0, behind[0])
+    path_ref[1, H:] = pad8(jnp.where(second, 0.0, behind[2]))
+    m, v, c = compose((early[:H], early_v, early_c), behind)
+    write_pack(
+        pack_ref,
+        m,
+        [v, c]
+        + [early[ROW_PROJ + p : ROW_PROJ + p + 1] for p in range(3)]
+        + [late[ROW_REC + p : ROW_REC + p + 1] for p in range(3)]
+        + [late[ROW_LAST : ROW_LAST + 1]],
+    )
+
+
 def reach_kernel(
     nodes_ref,
     links1_ref,
-    links2_ref,
+    path2_ref,
+    path3_ref,
     wrec_ref,
     maps_hbm,
     vecs_hbm,
@@ -382,9 +421,10 @@
     ut_ref,
     sems,
 ):
-    _, middle, near = places()
-    to1, back1 = paths_to(near, links1_ref)
-    to2, back2 = paths_to(middle, links2_ref)
+    to, back = paths_to(places()[1], links1_ref)
+    for path_ref in (path2_ref, path3_ref):
+        to = forward_join((path_ref[0, :H], path_ref[0, H : H + 1]), to)
+        back = adjoint_join(back, (path_ref[1, :H], path_ref[1, H : H + 1]))
     none = (jnp.zeros((H, H), F32), jnp.zeros((1, H), F32))
 
     def put(slot, found, flip):
@@ -392,8 +432,8 @@
         maps_ref[slot] = halves(m.T if flip else m)
         vecs_ref[slot : slot + 1] = v
 
-    put(2 * BLOCKS, forward_join(to2, to1), False)
-    put(2 * BLOCKS + 1, adjoint_join(back1, back2), True)
+    put(2 * BLOCKS, to, False)
+    put(2 * BLOCKS + 1, back, True)
     vecs_ref[2 * BLOCKS + 2 :] = jnp.zeros((6, H), F32)
 
     def node(n, row):
@@ -534,13 +574,8 @@
 
 def group_lists(count):
     near = [list(range(s, s + 4)) for s in range(0, count, 4)]
-    middle = [
-        [16 * y + i, 16 * y + 4 + i, 16 * y + 11 - i, 16 * y + 15 - i]
-        for y in range(count // 16)
-        for i in range(4)
-    ]
     far = [[16 * y + z for y in range(4)] for z in range(16)]
-    return near, middle, far
+    return near, far
 
 
 def shape(*dims):
@@ -550,7 +585,8 @@
 def per_device(
     inputs, trajectory, initial_state, cotangent, in_weight, recurrent_weight, gate_bias
 ):
-    near, middle, far = group_lists(lax.axis_size("seq"))
+    count = lax.axis_size("seq")
+    near, far = group_lists(count)
     pack, nodes, steps = call(
         local_kernel,
         (
@@ -584,14 +620,25 @@
         gate_bias,
     )
     merge = call(
-        merge_kernel, (shape(4, ROWS, H), shape(6, H + 8, H)), 10**8, "vv", "vv"
+        merge_kernel, (shape(1, ROWS, H), shape(6, H + 8, H)), 10**8, "vv", "vv"
     )
 
     def exchange(packed, groups):
         return lax.all_to_all(packed, "seq", 0, 0, axis_index_groups=groups)
 
+    def pair(packed, bit, flip, copies):
+        other = lax.ppermute(packed, "seq", [(i, i ^ flip) for i in range(count)])
+        return call(
+            functools.partial(pair_kernel, bit=bit),
+            (shape(copies, ROWS, H), shape(2, H + 8, H)),
+            10**8,
+            "vvv",
+            "vv",
+        )(packed, other, recurrent_weight)
+
     pack, links1 = merge(exchange(pack, near), recurrent_weight)
-    pack, links2 = merge(exchange(pack, middle), recurrent_weight)
+    pack, path2 = pair(pack, 4, 4, 1)
+    pack, path3 = pair(pack, 8, 12, 4)
     group = exchange(pack, far)
     found = (
         (2 * BLOCKS + 2, H, 2 * H),
@@ -605,10 +652,10 @@
         reach_kernel,
         tuple(jax.ShapeDtypeStruct(dims, kind) for dims, kind in zip(found, kinds)),
         5 * 10**8,
-        "vvvv",
+        "vvvvv",
         "hhhh",
         buffers + [pltpu.SemaphoreType.DMA((4,))],
-    )(nodes, links1, links2, recurrent_weight)
+    )(nodes, links1, path2, path3, recurrent_weight)
     new_state, adjoint = call(
         apply_kernel,
         (shape(1, H, H), shape(1, H, H)),

time: 71.8 us -> 67 us (0.933)
  the two profiles are of different devices: /device:TPU:6 before, /device:TPU:98 now
where the time goes in v4:
time: 67 us; the launch traced here: 66.7 us
  starting transfers between devices  22.9 us (34%)
  Pallas kernels  17.1 us (26%)
  waiting for transfers between devices  13.9 us (21%)
  blocking collectives  12.1 us (18%)
  between operations  0.69 us (1%)
    ppermute x2, starting transfers between devices, pair(): other = lax.ppermute(packed, 'seq', [(i, i ^ flip) for i in range(count)])  18.4 us
    pallas_call x6, Pallas kernels, placed(): run(*(pltpu.with_memory_space_constraint(a, pltpu.HBM) if k == 'h' else a...  17.1 us
    all_to_all x1, blocking collectives, exchange(): return lax.all_to_all(packed, 'seq', 0, 0, axis_index_groups=groups)  12.1 us
    ppermute x2, waiting for transfers between devices, pair(): other = lax.ppermute(packed, 'seq', [(i, i ^ flip) for i in range(count)])  9.67 us
    all_to_all x1, starting transfers between devices, exchange(): return lax.all_to_all(packed, 'seq', 0, 0, axis_index_groups=groups)  4.47 us
    all_to_all x1, waiting for transfers between devices, exchange(): return lax.all_to_all(packed, 'seq', 0, 0, axis_index_groups=groups)  4.2 us
  transfers between devices with their start and end apart: 3, of which 3 were waited for; matrix products, arithmetic and copies ran while one was open for 0% of the time, Pallas kernels for 5%

profile of v4, /device:TPU:98, one launch (start us, length us, event | category | flops | bytes accessed | tf_op | source)
XLA Modules:
  0.0 66.7 jit_solution(7341808767194341146)
XLA Ops:
  0.6 0.0 copy-start
  0.6 7.8 %shard_map.86 = (f32[4,144,128]{2,1,0:T(8,128)S(1)}, f32[32,136,128]{2,1,0:T(8,128)S(1)}, f32[5,128,128]{2,1,0:T(8,128)}) custom-call(f32[1,128,128]{2,1,0:T(8,128)} %x_hbm.1, f32[1,128,128]{2,1,0:T(8,128)} %traj_hbm.1, f32[1,128,128]{2,1,0:T(8,128)} %cot_hbm.3, f32[1,128]{1,0:T(1,128)} %init_hbm.3, f32[128,384]{1,0:T(8,128)} %win_hbm.1, ...), custom_call_target="tpu_custom_call" | custom-call | flops 2000000000 | bytes 1048576 | tf_op jit(solution)/shard_map/pallas_call | solution.py:565
  8.4 12.1 %all_to_all.10.group_ref = f32[4,144,128]{2,1,0:T(8,128)S(1)} all-to-all(f32[4,144,128]{2,1,0:T(8,128)S(1)} %get-tuple-element.15), channel_id=1, replica_groups={{0,1,2,3},{4,5,6,7},{8,9,10,11},{12,13,14,15},{16,17,18,19},{20,21,22,2..., dimensions={0} | all-to-all | bytes 589824 | tf_op jit(solution)/shard_map/all_to_all | solution.py:627
  20.5 0.0 copy-done
  20.5 0.7 %shard_map.87 = (f32[1,144,128]{2,1,0:T(8,128)S(1)}, f32[6,136,128]{2,1,0:T(8,128)S(1)}) custom-call(f32[4,144,128]{2,1,0:T(8,128)S(1)} %all_to_all.10.group_ref, f32[128,384]{1,0:T(8,128)S(1)} %copy-done), custom_call_target="tpu_custom_call" | custom-call | flops 100000000 | bytes 1048576 | tf_op jit(solution)/shard_map/pallas_call | solution.py:565
  21.2 9.1 %collective-permute-start = (f32[1,144,128]{2,1,0:T(8,128)S(1)}, f32[1,144,128]{2,1,0:T(8,128)S(1)}, u32[]{:S(2)}, u32[]{:S(2)}) collective-permute-start(f32[1,144,128]{2,1,0:T(8,128)S(1)} %get-tuple-element.16.own_ref), channel_id=1, source_target_pairs={{0,4},{1,5},{2,6},{3,7},{4,0},{5,1},{6,2},{7,3},{8,12},{9,13},{10,... | collective-permute-start | bytes 221192 | tf_op jit(solution)/shard_map/ppermute | solution.py:630
  30.3 5.3 %collective-permute-done.other_ref = f32[1,144,128]{2,1,0:T(8,128)S(1)} collective-permute-done((f32[1,144,128]{2,1,0:T(8,128)S(1)}, f32[1,144,128]{2,1,0:T(8,128)S(1)}, u32[]{:S(2)}, u32[]{:S(2)}) %collective-permute-start) | collective-permute-done | bytes 73760 | tf_op jit(solution)/shard_map/ppermute | solution.py:630
  35.6 0.4 shard_map.88
  36.0 9.3 %collective-permute-start.1 = (f32[1,144,128]{2,1,0:T(8,128)S(1)}, f32[1,144,128]{2,1,0:T(8,128)S(1)}, u32[]{:S(2)}, u32[]{:S(2)}) collective-permute-start(f32[1,144,128]{2,1,0:T(8,128)S(1)} %get-tuple-element.17.own_ref), channel_id=1, source_target_pairs={{0,12},{1,13},{2,14},{3,15},{4,8},{5,9},{6,10},{7,11},{8,4},{9,5},... | collective-permute-start | bytes 221192 | tf_op jit(solution)/shard_map/ppermute | solution.py:630
  45.3 4.4 %collective-permute-done.1.other_ref = f32[1,144,128]{2,1,0:T(8,128)S(1)} collective-permute-done((f32[1,144,128]{2,1,0:T(8,128)S(1)}, f32[1,144,128]{2,1,0:T(8,128)S(1)}, u32[]{:S(2)}, u32[]{:S(2)}) %collective-permute-start.1) | collective-permute-done | bytes 73760 | tf_op jit(solution)/shard_map/ppermute | solution.py:630
  49.7 1.1 %shard_map.89 = (f32[4,144,128]{2,1,0:T(8,128)}, f32[2,136,128]{2,1,0:T(8,128)S(1)}) custom-call(f32[1,144,128]{2,1,0:T(8,128)S(1)} %get-tuple-element.17.own_ref, f32[1,144,128]{2,1,0:T(8,128)S(1)} %collective-permute-done.1.other_ref, f32[128,384]{1,0:T(8,128)S(1)} %copy-done), custom_call_target="tpu_custom_call" | custom-call | flops 100000000 | bytes 1048576 | tf_op jit(solution)/shard_map/pallas_call | solution.py:565
  50.8 4.5 %all-to-all-start.1 = ((f32[4,144,128]{2,1,0:T(8,128)}), f32[4,144,128]{2,1,0:T(8,128)S(1)}, u32[]{:S(2)}, u32[]{:S(2)}) async-start(f32[4,144,128]{2,1,0:T(8,128)} %get-tuple-element.18), calls=%async_computation.1 | async-start | bytes 589824 | tf_op jit(solution)/shard_map/all_to_all | solution.py:627
  55.3 3.0 %shard_map.90 = (bf16[34,128,256]{2,1,0:T(8,128)(2,1)}, f32[40,128]{1,0:T(8,128)}, bf16[128,768]{1,0:T(8,128)(2,1)}, bf16[384,256]{1,0:T(8,128)(2,1)}) custom-call(f32[32,136,128]{2,1,0:T(8,128)S(1)} %get-tuple-element.19.nodes_ref, f32[6,136,128]{2,1,0:T(8,128)S(1)} %get-tuple-element.20.links1_ref, f32[2,136,128]{2,1,0:T(8,128)S(1)} %get-tuple-element.21.path2_ref, ...), custom_call_target="tpu_custom_call" | custom-call | flops 500000000 | bytes 1048576 | tf_op jit(solution)/shard_map/pallas_call | solution.py:565
  58.3 4.2 %all-to-all-done.1.group_ref = f32[4,144,128]{2,1,0:T(8,128)S(1)} async-done(((f32[4,144,128]{2,1,0:T(8,128)}), f32[4,144,128]{2,1,0:T(8,128)S(1)}, u32[]{:S(2)}, u32[]{:S(2)}) %all-to-all-start.1) | async-done | bytes 294944 | tf_op jit(solution)/shard_map/all_to_all | solution.py:627
  62.5 4.2 %shard_map.91 = (f32[1,128,128]{2,1,0:T(8,128)}, f32[1,128,128]{2,1,0:T(8,128)}) custom-call(f32[4,144,128]{2,1,0:T(8,128)S(1)} %all-to-all-done.1.group_ref, f32[32,136,128]{2,1,0:T(8,128)S(1)} %get-tuple-element.19.nodes_ref, f32[128,384]{1,0:T(8,128)S(1)} %copy-done, bf16[34,128,256]{2,1,0:T(8,128)(2,1)} %get-tuple-element.23.maps_hbm, ...), custom_call_target="tpu_custom_call" | custom-call | flops 100000000 | bytes 1048576 | tf_op jit(solution)/shard_map/pallas_call | solution.py:565
Async XLA Ops:
  0.6 19.9 %copy-start = (f32[128,384]{1,0:T(8,128)S(1)}, f32[128,384]{1,0:T(8,128)}, u32[]{:S(2)}) copy-start(f32[128,384]{1,0:T(8,128)} %wrec_ref.9) | copy-start | bytes 589828
  21.2 14.4 %collective-permute-start = (f32[1,144,128]{2,1,0:T(8,128)S(1)}, f32[1,144,128]{2,1,0:T(8,128)S(1)}, u32[]{:S(2)}, u32[]{:S(2)}) collective-permute-start(f32[1,144,128]{2,1,0:T(8,128)S(1)} %get-tuple-element.16.own_ref), channel_id=1, source_target_pairs={{0,4},{1,5},{2,6},{3,7},{4,0},{5,1},{6,2},{7,3},{8,12},{9,13},{10,... | collective-permute-start | bytes 221192 | tf_op jit(solution)/shard_map/ppermute | solution.py:630
  36.0 13.7 %collective-permute-start.1 = (f32[1,144,128]{2,1,0:T(8,128)S(1)}, f32[1,144,128]{2,1,0:T(8,128)S(1)}, u32[]{:S(2)}, u32[]{:S(2)}) collective-permute-start(f32[1,144,128]{2,1,0:T(8,128)S(1)} %get-tuple-element.17.own_ref), channel_id=1, source_target_pairs={{0,12},{1,13},{2,14},{3,15},{4,8},{5,9},{6,10},{7,11},{8,4},{9,5},... | collective-permute-start | bytes 221192 | tf_op jit(solution)/shard_map/ppermute | solution.py:630
  50.8 11.7 %all-to-all-start.1 = ((f32[4,144,128]{2,1,0:T(8,128)}), f32[4,144,128]{2,1,0:T(8,128)S(1)}, u32[]{:S(2)}, u32[]{:S(2)}) async-start(f32[4,144,128]{2,1,0:T(8,128)} %get-tuple-element.18), calls=%async_computation.1 | async-start | bytes 589824 | tf_op jit(solution)/shard_map/all_to_all | solution.py:627

commit v5 on v4

--- a/solution.py
+++ b/solution.py
@@ -65,10 +65,7 @@
 
 
 def vec_mm_t(row, b):
-    out = lax.dot_general(
-        stacked(pad8(row)), stacked(b), (((1,), (1,)), ((), ())), preferred_element_type=F32
-    )
-    return both_halves(out[:8] + out[8:])[:1]
+    return vec_mm(row, b.T)
 
 
 def eye():
@@ -226,7 +223,9 @@
         m, v, c = compose(node(2 * n), node(2 * n + 1))
         nodes_ref[n, :H] = m
         nodes_ref[n, H:] = two_rows(v, c)
-    nodes_ref[0, :8] = jnp.concatenate([*parts3(rec_init), jnp.zeros((5, H), F32)], axis=0)
+    nodes_ref[0, :8] = jnp.concatenate(
+        [*parts3(rec_init), init_ref[...], jnp.zeros((4, H), F32)], axis=0
+    )
     nodes_ref[0, 8:] = jnp.zeros((H, H), F32)
     m, v, c = node(1)
     rec_last = rec_rows[H - 1 : H]
@@ -406,7 +405,6 @@
 
 
 def reach_kernel(
-    nodes_ref,
     links1_ref,
     path2_ref,
     path3_ref,
@@ -425,31 +423,15 @@
     for path_ref in (path2_ref, path3_ref):
         to = forward_join((path_ref[0, :H], path_ref[0, H : H + 1]), to)
         back = adjoint_join(back, (path_ref[1, :H], path_ref[1, H : H + 1]))
-    none = (jnp.zeros((H, H), F32), jnp.zeros((1, H), F32))
 
     def put(slot, found, flip):
-        m, v = found or none
+        m, v = found
         maps_ref[slot] = halves(m.T if flip else m)
         vecs_ref[slot : slot + 1] = v
 
-    put(2 * BLOCKS, to, False)
-    put(2 * BLOCKS + 1, back, True)
-    vecs_ref[2 * BLOCKS + 2 :] = jnp.zeros((6, H), F32)
-
-    def node(n, row):
-        return nodes_ref[n, :H], nodes_ref[n, H + row : H + row + 1]
-
-    before, after = {1: None}, {1: None}
-    for n in range(1, BLOCKS):
-        before[2 * n] = before[n]
-        first = node(2 * n, 0)
-        before[2 * n + 1] = first if before[n] is None else forward_join(before[n], first)
-        after[2 * n + 1] = after[n]
-        last = node(2 * n + 1, 1)
-        after[2 * n] = last if after[n] is None else adjoint_join(last, after[n])
-    for k in range(BLOCKS):
-        put(k, before[BLOCKS + k], False)
-        put(BLOCKS + k, after[BLOCKS + k], True)
+    put(0, to, False)
+    put(1, back, True)
+    vecs_ref[2:] = jnp.zeros((6, H), F32)
     u = wrec_ref[...]
     u_ref[...] = halves(u)
     ut_ref[...] = halves(u.T)
@@ -479,7 +461,6 @@
     ut_hbm,
     steps_hbm,
     cot_hbm,
-    init_hbm,
     state_ref,
     adjoint_ref,
     maps_ref,
@@ -488,14 +469,12 @@
     ut_ref,
     steps_ref,
     cot_ref,
-    init_ref,
     sems,
 ):
     copies = [
         pltpu.make_async_copy(src, dst, sems.at[i])
         for i, (src, dst) in enumerate(
             (
-                (init_hbm, init_ref),
                 (maps_hbm, maps_ref),
                 (vecs_hbm, vecs_ref),
                 (u_hbm, u_ref),
@@ -509,8 +488,7 @@
         copy.start()
     per_block = H // BLOCKS
     ahead, behind = links(group_ref, wrec_ref)
-    copies[0].wait()
-    init = init_ref[...]
+    init = nodes_ref[0, 3:4]
     rec = [nodes_ref[0, p : p + 1] for p in range(3)]
     write, terms, off = gates(
         [group_ref[0, ROW_PROJ + p : ROW_PROJ + p + 1] for p in range(3)], rec, init
@@ -529,15 +507,26 @@
         i = 2 - j
         moved = costate + vec_mm_t(costate, behind[i][0]) + behind[i][2]
         costate = jnp.where(i >= own, moved, costate)
-    for copy in copies[1:]:
+    for copy in copies[:2]:
         copy.wait()
-    at = 2 * BLOCKS
-    state = state + moved_by(state, maps_ref[at]) + vecs_ref[at : at + 1]
-    costate = costate + moved_by(costate, maps_ref[at + 1]) + vecs_ref[at + 1 : at + 2]
-    fwd = jnp.concatenate([moved_by(state, maps_ref[k]) for k in range(BLOCKS)], axis=0)
-    fwd = state + fwd + vecs_ref[:BLOCKS]
-    bwd = jnp.concatenate([moved_by(costate, maps_ref[BLOCKS + k]) for k in range(BLOCKS)], axis=0)
-    bwd = costate + bwd + vecs_ref[BLOCKS : 2 * BLOCKS]
+    states = {1: state + moved_by(state, maps_ref[0]) + vecs_ref[0:1]}
+    costates = {1: costate + moved_by(costate, maps_ref[1]) + vecs_ref[1:2]}
+    for n in range(1, BLOCKS):
+        state, costate = states[n], costates[n]
+        states[2 * n] = state
+        states[2 * n + 1] = (
+            state + vec_mm(state, nodes_ref[2 * n, :H]) + nodes_ref[2 * n, H : H + 1]
+        )
+        costates[2 * n] = (
+            costate
+            + vec_mm_t(costate, nodes_ref[2 * n + 1, :H])
+            + nodes_ref[2 * n + 1, H + 1 : H + 2]
+        )
+        costates[2 * n + 1] = costate
+    fwd = jnp.concatenate([states[BLOCKS + k] for k in range(BLOCKS)], axis=0)
+    bwd = jnp.concatenate([costates[BLOCKS + k] for k in range(BLOCKS)], axis=0)
+    for copy in copies[2:]:
+        copy.wait()
     u_side, u_back = u_ref[...], ut_ref[...]
     for l in range(per_block):
         fwd = forward_step(fwd, steps_ref, l, u_side, per_block)
@@ -637,12 +626,12 @@
         )(packed, other, recurrent_weight)
 
     pack, links1 = merge(exchange(pack, near), recurrent_weight)
-    pack, path2 = pair(pack, 4, 4, 1)
+    pack, path2 = pair(pack, 4, 7, 1)
     pack, path3 = pair(pack, 8, 12, 4)
     group = exchange(pack, far)
     found = (
-        (2 * BLOCKS + 2, H, 2 * H),
-        (2 * BLOCKS + 8, H),
+        (2, H, 2 * H),
+        (8, H),
         (H, 6 * H),
         (3 * H, 2 * H),
     )
@@ -651,25 +640,24 @@
     reached = call(
         reach_kernel,
         tuple(jax.ShapeDtypeStruct(dims, kind) for dims, kind in zip(found, kinds)),
-        5 * 10**8,
-        "vvvvv",
+        10**8,
+        "vvvv",
         "hhhh",
         buffers + [pltpu.SemaphoreType.DMA((4,))],
-    )(nodes, links1, path2, path3, recurrent_weight)
+    )(links1, path2, path3, recurrent_weight)
     new_state, adjoint = call(
         apply_kernel,
         (shape(1, H, H), shape(1, H, H)),
         10**8,
-        "vvvhhhhhhh",
+        "vvvhhhhhh",
         "vv",
         buffers
         + [
             pltpu.VMEM((5, H, H), F32),
             pltpu.VMEM((1, H, H), F32),
-            pltpu.VMEM((1, H), F32),
-            pltpu.SemaphoreType.DMA((7,)),
+            pltpu.SemaphoreType.DMA((6,)),
         ],
-    )(group, nodes, recurrent_weight, *reached, steps, cotangent, initial_state)
+    )(group, nodes, recurrent_weight, *reached, steps, cotangent)
     return new_state, adjoint
 
 

time: 67 us -> 65.9 us (0.984)
  the two profiles are of different devices: /device:TPU:98 before, /device:TPU:6 now
where the time goes in v5:
time: 65.9 us; the launch traced here: 65.6 us
  starting transfers between devices  23 us (35%)
  Pallas kernels  15.5 us (24%)
  blocking collectives  15.3 us (23%)
  waiting for transfers between devices  11.1 us (17%)
  between operations  0.68 us (1%)
    ppermute x2, starting transfers between devices, pair(): other = lax.ppermute(packed, 'seq', [(i, i ^ flip) for i in range(count)])  18.5 us
    pallas_call x6, Pallas kernels, placed(): run(*(pltpu.with_memory_space_constraint(a, pltpu.HBM) if k == 'h' else a...  15.5 us
    all_to_all x1, blocking collectives, exchange(): return lax.all_to_all(packed, 'seq', 0, 0, axis_index_groups=groups)  15.3 us
    ppermute x2, waiting for transfers between devices, pair(): other = lax.ppermute(packed, 'seq', [(i, i ^ flip) for i in range(count)])  5.83 us
    all_to_all x1, waiting for transfers between devices, exchange(): return lax.all_to_all(packed, 'seq', 0, 0, axis_index_groups=groups)  5.29 us
    all_to_all x1, starting transfers between devices, exchange(): return lax.all_to_all(packed, 'seq', 0, 0, axis_index_groups=groups)  4.47 us
  transfers between devices with their start and end apart: 3, of which 3 were waited for; matrix products, arithmetic and copies ran while one was open for 0% of the time, Pallas kernels for 2%

profile of v5, /device:TPU:6, one launch (start us, length us, event | category | flops | bytes accessed | tf_op | source)
XLA Modules:
  0.0 65.6 jit_solution(2247515207850370123)
XLA Ops:
  0.6 0.0 copy-start
  0.6 7.8 %shard_map.86 = (f32[4,144,128]{2,1,0:T(8,128)S(1)}, f32[32,136,128]{2,1,0:T(8,128)S(1)}, f32[5,128,128]{2,1,0:T(8,128)}) custom-call(f32[1,128,128]{2,1,0:T(8,128)} %x_hbm.1, f32[1,128,128]{2,1,0:T(8,128)} %traj_hbm.1, f32[1,128,128]{2,1,0:T(8,128)} %cot_hbm.3, f32[1,128]{1,0:T(1,128)} %init_hbm.1, f32[128,384]{1,0:T(8,128)} %win_hbm.1, ...), custom_call_target="tpu_custom_call" | custom-call | flops 2000000000 | bytes 1048576 | tf_op jit(solution)/shard_map/pallas_call | solution.py:554
  8.5 15.3 %all_to_all.10.group_ref = f32[4,144,128]{2,1,0:T(8,128)S(1)} all-to-all(f32[4,144,128]{2,1,0:T(8,128)S(1)} %get-tuple-element.15), channel_id=1, replica_groups={{0,1,2,3},{4,5,6,7},{8,9,10,11},{12,13,14,15},{16,17,18,19},{20,21,22,2..., dimensions={0} | all-to-all | bytes 589824 | tf_op jit(solution)/shard_map/all_to_all | solution.py:616
  23.8 0.0 copy-done
  23.8 0.7 %shard_map.87 = (f32[1,144,128]{2,1,0:T(8,128)S(1)}, f32[6,136,128]{2,1,0:T(8,128)S(1)}) custom-call(f32[4,144,128]{2,1,0:T(8,128)S(1)} %all_to_all.10.group_ref, f32[128,384]{1,0:T(8,128)S(1)} %copy-done), custom_call_target="tpu_custom_call" | custom-call | flops 100000000 | bytes 1048576 | tf_op jit(solution)/shard_map/pallas_call | solution.py:554
  24.5 10.0 %collective-permute-start = (f32[1,144,128]{2,1,0:T(8,128)S(1)}, f32[1,144,128]{2,1,0:T(8,128)S(1)}, u32[]{:S(2)}, u32[]{:S(2)}) collective-permute-start(f32[1,144,128]{2,1,0:T(8,128)S(1)} %get-tuple-element.16.own_ref), channel_id=1, source_target_pairs={{0,7},{1,6},{2,5},{3,4},{4,3},{5,2},{6,1},{7,0},{8,15},{9,14},{10,... | collective-permute-start | bytes 221192 | tf_op jit(solution)/shard_map/ppermute | solution.py:619
  34.5 2.9 %collective-permute-done.other_ref = f32[1,144,128]{2,1,0:T(8,128)S(1)} collective-permute-done((f32[1,144,128]{2,1,0:T(8,128)S(1)}, f32[1,144,128]{2,1,0:T(8,128)S(1)}, u32[]{:S(2)}, u32[]{:S(2)}) %collective-permute-start) | collective-permute-done | bytes 73760 | tf_op jit(solution)/shard_map/ppermute | solution.py:619
  37.4 0.4 shard_map.88
  37.8 8.5 %collective-permute-start.1 = (f32[1,144,128]{2,1,0:T(8,128)S(1)}, f32[1,144,128]{2,1,0:T(8,128)S(1)}, u32[]{:S(2)}, u32[]{:S(2)}) collective-permute-start(f32[1,144,128]{2,1,0:T(8,128)S(1)} %get-tuple-element.17.own_ref), channel_id=1, source_target_pairs={{0,12},{1,13},{2,14},{3,15},{4,8},{5,9},{6,10},{7,11},{8,4},{9,5},... | collective-permute-start | bytes 221192 | tf_op jit(solution)/shard_map/ppermute | solution.py:619
  46.3 2.9 %collective-permute-done.1.other_ref = f32[1,144,128]{2,1,0:T(8,128)S(1)} collective-permute-done((f32[1,144,128]{2,1,0:T(8,128)S(1)}, f32[1,144,128]{2,1,0:T(8,128)S(1)}, u32[]{:S(2)}, u32[]{:S(2)}) %collective-permute-start.1) | collective-permute-done | bytes 73760 | tf_op jit(solution)/shard_map/ppermute | solution.py:619
  49.3 1.1 %shard_map.89 = (f32[4,144,128]{2,1,0:T(8,128)}, f32[2,136,128]{2,1,0:T(8,128)S(1)}) custom-call(f32[1,144,128]{2,1,0:T(8,128)S(1)} %get-tuple-element.17.own_ref, f32[1,144,128]{2,1,0:T(8,128)S(1)} %collective-permute-done.1.other_ref, f32[128,384]{1,0:T(8,128)S(1)} %copy-done), custom_call_target="tpu_custom_call" | custom-call | flops 100000000 | bytes 1048576 | tf_op jit(solution)/shard_map/pallas_call | solution.py:554
  50.4 4.5 %all-to-all-start.1 = ((f32[4,144,128]{2,1,0:T(8,128)}), f32[4,144,128]{2,1,0:T(8,128)S(1)}, u32[]{:S(2)}, u32[]{:S(2)}) async-start(f32[4,144,128]{2,1,0:T(8,128)} %get-tuple-element.18), calls=%async_computation.1 | async-start | bytes 589824 | tf_op jit(solution)/shard_map/all_to_all | solution.py:616
  54.9 1.6 %shard_map.90 = (bf16[2,128,256]{2,1,0:T(8,128)(2,1)}, f32[8,128]{1,0:T(8,128)}, bf16[128,768]{1,0:T(8,128)(2,1)}, bf16[384,256]{1,0:T(8,128)(2,1)}) custom-call(f32[6,136,128]{2,1,0:T(8,128)S(1)} %get-tuple-element.20.links1_ref, f32[2,136,128]{2,1,0:T(8,128)S(1)} %get-tuple-element.21.path2_ref, f32[2,136,128]{2,1,0:T(8,128)S(1)} %get-tuple-element.22.path3_ref, ...), custom_call_target="tpu_custom_call" | custom-call | flops 100000000 | bytes 1048576 | tf_op jit(solution)/shard_map/pallas_call | solution.py:554
  56.4 5.3 %all-to-all-done.1.group_ref = f32[4,144,128]{2,1,0:T(8,128)S(1)} async-done(((f32[4,144,128]{2,1,0:T(8,128)}), f32[4,144,128]{2,1,0:T(8,128)S(1)}, u32[]{:S(2)}, u32[]{:S(2)}) %all-to-all-start.1) | async-done | bytes 294944 | tf_op jit(solution)/shard_map/all_to_all | solution.py:616
  61.7 3.8 %shard_map.91 = (f32[1,128,128]{2,1,0:T(8,128)}, f32[1,128,128]{2,1,0:T(8,128)}) custom-call(f32[4,144,128]{2,1,0:T(8,128)S(1)} %all-to-all-done.1.group_ref, f32[32,136,128]{2,1,0:T(8,128)S(1)} %get-tuple-element.19.nodes_ref, f32[128,384]{1,0:T(8,128)S(1)} %copy-done, bf16[2,128,256]{2,1,0:T(8,128)(2,1)} %get-tuple-element.23.maps_hbm, ...), custom_call_target="tpu_custom_call" | custom-call | flops 100000000 | bytes 1048576 | tf_op jit(solution)/shard_map/pallas_call | solution.py:554
Async XLA Ops:
  0.6 23.1 %copy-start = (f32[128,384]{1,0:T(8,128)S(1)}, f32[128,384]{1,0:T(8,128)}, u32[]{:S(2)}) copy-start(f32[128,384]{1,0:T(8,128)} %wrec_ref.9) | copy-start | bytes 589828
  24.5 12.9 %collective-permute-start = (f32[1,144,128]{2,1,0:T(8,128)S(1)}, f32[1,144,128]{2,1,0:T(8,128)S(1)}, u32[]{:S(2)}, u32[]{:S(2)}) collective-permute-start(f32[1,144,128]{2,1,0:T(8,128)S(1)} %get-tuple-element.16.own_ref), channel_id=1, source_target_pairs={{0,7},{1,6},{2,5},{3,4},{4,3},{5,2},{6,1},{7,0},{8,15},{9,14},{10,... | collective-permute-start | bytes 221192 | tf_op jit(solution)/shard_map/ppermute | solution.py:619
  37.8 11.5 %collective-permute-start.1 = (f32[1,144,128]{2,1,0:T(8,128)S(1)}, f32[1,144,128]{2,1,0:T(8,128)S(1)}, u32[]{:S(2)}, u32[]{:S(2)}) collective-permute-start(f32[1,144,128]{2,1,0:T(8,128)S(1)} %get-tuple-element.17.own_ref), channel_id=1, source_target_pairs={{0,12},{1,13},{2,14},{3,15},{4,8},{5,9},{6,10},{7,11},{8,4},{9,5},... | collective-permute-start | bytes 221192 | tf_op jit(solution)/shard_map/ppermute | solution.py:619
  50.4 11.3 %all-to-all-start.1 = ((f32[4,144,128]{2,1,0:T(8,128)}), f32[4,144,128]{2,1,0:T(8,128)S(1)}, u32[]{:S(2)}, u32[]{:S(2)}) async-start(f32[4,144,128]{2,1,0:T(8,128)} %get-tuple-element.18), calls=%async_computation.1 | async-start | bytes 589824 | tf_op jit(solution)/shard_map/all_to_all | solution.py:616

commit v6 on v5

--- a/solution.py
+++ b/solution.py
@@ -65,7 +65,10 @@
 
 
 def vec_mm_t(row, b):
-    return vec_mm(row, b.T)
+    out = lax.dot_general(
+        stacked(pad8(row)), stacked(b), (((1,), (1,)), ((), ())), preferred_element_type=F32
+    )
+    return both_halves(out[:8] + out[8:])[:1]
 
 
 def eye():
@@ -313,15 +316,9 @@
     return ahead, behind
 
 
-def merge_kernel(group_ref, wrec_ref, pack_ref, links_ref):
+def merge_kernel(group_ref, wrec_ref, pack_ref, path_ref):
     ahead, behind = links(group_ref, wrec_ref)
-    for j in range(3):
-        m, v = ahead[j]
-        links_ref[j, :H] = m
-        links_ref[j, H:] = pad8(v)
-        m, v, c = behind[j]
-        links_ref[3 + j, :H] = m
-        links_ref[3 + j, H:] = pad8(c)
+    put_path(path_ref, *paths_to(places()[1], ahead, [(m, c) for m, _, c in behind]))
     start = (
         group_ref[0, :H],
         group_ref[0, ROW_B : ROW_B + 1],
@@ -355,9 +352,7 @@
     )
 
 
-def paths_to(own, links_ref):
-    ahead = [(links_ref[j, :H], links_ref[j, H : H + 1]) for j in range(3)]
-    behind = [(links_ref[3 + j, :H], links_ref[3 + j, H : H + 1]) for j in range(3)]
+def paths_to(own, ahead, behind):
     keep = lambda on, new, old: tuple(jnp.where(on, n, o) for n, o in zip(new, old))
     none = (jnp.zeros((H, H), F32), jnp.zeros((1, H), F32))
     to = keep(own > 0, ahead[0], none)
@@ -368,7 +363,13 @@
     return to, back
 
 
-def pair_kernel(own_ref, other_ref, wrec_ref, pack_ref, path_ref, *, bit):
+def put_path(path_ref, to, back):
+    for i, (m, v) in enumerate((to, back)):
+        path_ref[i, :H] = m
+        path_ref[i, H:] = pad8(v)
+
+
+def pair_kernel(own_ref, other_ref, inner_ref, wrec_ref, pack_ref, path_ref, *, bit):
     second = lax.axis_index("seq") // bit % 2 == 1
     own, other = own_ref[0], other_ref[0]
     early = jnp.where(second, other, own)
@@ -389,10 +390,13 @@
         off + prod[H : H + 1] + late_v,
         late_c + vec_mm_t(late_c, first),
     )
-    path_ref[0, :H] = jnp.where(second, ahead[0], 0.0)
-    path_ref[0, H:] = pad8(jnp.where(second, ahead[1], 0.0))
-    path_ref[1, :H] = jnp.where(second, 0.0, behind[0])
-    path_ref[1, H:] = pad8(jnp.where(second, 0.0, behind[2]))
+    to = tuple(jnp.where(second, a, 0.0) for a in ahead)
+    back = tuple(jnp.where(second, 0.0, a) for a in (behind[0], behind[2]))
+    put_path(
+        path_ref,
+        forward_join(to, (inner_ref[0, :H], inner_ref[0, H : H + 1])),
+        adjoint_join((inner_ref[1, :H], inner_ref[1, H : H + 1]), back),
+    )
     m, v, c = compose((early[:H], early_v, early_c), behind)
     write_pack(
         pack_ref,
@@ -404,85 +408,22 @@
     )
 
 
-def reach_kernel(
-    links1_ref,
-    path2_ref,
-    path3_ref,
-    wrec_ref,
-    maps_hbm,
-    vecs_hbm,
-    u_hbm,
-    ut_hbm,
-    maps_ref,
-    vecs_ref,
-    u_ref,
-    ut_ref,
-    sems,
-):
-    to, back = paths_to(places()[1], links1_ref)
-    for path_ref in (path2_ref, path3_ref):
-        to = forward_join((path_ref[0, :H], path_ref[0, H : H + 1]), to)
-        back = adjoint_join(back, (path_ref[1, :H], path_ref[1, H : H + 1]))
-
-    def put(slot, found, flip):
-        m, v = found
-        maps_ref[slot] = halves(m.T if flip else m)
-        vecs_ref[slot : slot + 1] = v
-
-    put(0, to, False)
-    put(1, back, True)
-    vecs_ref[2:] = jnp.zeros((6, H), F32)
-    u = wrec_ref[...]
-    u_ref[...] = halves(u)
-    ut_ref[...] = halves(u.T)
-    copies = [
-        pltpu.make_async_copy(src, dst, sems.at[i])
-        for i, (src, dst) in enumerate(
-            ((maps_ref, maps_hbm), (vecs_ref, vecs_hbm), (u_ref, u_hbm), (ut_ref, ut_hbm))
-        )
-    ]
-    for copy in copies:
-        copy.start()
-    for copy in copies:
-        copy.wait()
-
-
-def moved_by(vector, weights):
-    return few_rows(pad8(vector), weights)[:1]
-
-
 def apply_kernel(
     group_ref,
+    path_ref,
     nodes_ref,
     wrec_ref,
-    maps_hbm,
-    vecs_hbm,
-    u_hbm,
-    ut_hbm,
     steps_hbm,
     cot_hbm,
     state_ref,
     adjoint_ref,
-    maps_ref,
-    vecs_ref,
-    u_ref,
-    ut_ref,
     steps_ref,
     cot_ref,
     sems,
 ):
     copies = [
-        pltpu.make_async_copy(src, dst, sems.at[i])
-        for i, (src, dst) in enumerate(
-            (
-                (maps_hbm, maps_ref),
-                (vecs_hbm, vecs_ref),
-                (u_hbm, u_ref),
-                (ut_hbm, ut_ref),
-                (steps_hbm, steps_ref),
-                (cot_hbm, cot_ref),
-            )
-        )
+        pltpu.make_async_copy(steps_hbm, steps_ref, sems.at[0]),
+        pltpu.make_async_copy(cot_hbm, cot_ref, sems.at[1]),
     ]
     for copy in copies:
         copy.start()
@@ -505,12 +446,10 @@
         moved = state + vec_mm(state, ahead[j][0]) + ahead[j][1]
         state = jnp.where(j < own, moved, state)
         i = 2 - j
-        moved = costate + vec_mm_t(costate, behind[i][0]) + behind[i][2]
+        moved = costate + vec_mm(costate, behind[i][0].T) + behind[i][2]
         costate = jnp.where(i >= own, moved, costate)
-    for copy in copies[:2]:
-        copy.wait()
-    states = {1: state + moved_by(state, maps_ref[0]) + vecs_ref[0:1]}
-    costates = {1: costate + moved_by(costate, maps_ref[1]) + vecs_ref[1:2]}
+    states = {1: state + vec_mm(state, path_ref[0, :H]) + path_ref[0, H : H + 1]}
+    costates = {1: costate + vec_mm(costate, path_ref[1, :H].T) + path_ref[1, H : H + 1]}
     for n in range(1, BLOCKS):
         state, costate = states[n], costates[n]
         states[2 * n] = state
@@ -519,15 +458,15 @@
         )
         costates[2 * n] = (
             costate
-            + vec_mm_t(costate, nodes_ref[2 * n + 1, :H])
+            + vec_mm(costate, nodes_ref[2 * n + 1, :H].T)
             + nodes_ref[2 * n + 1, H + 1 : H + 2]
         )
         costates[2 * n + 1] = costate
     fwd = jnp.concatenate([states[BLOCKS + k] for k in range(BLOCKS)], axis=0)
     bwd = jnp.concatenate([costates[BLOCKS + k] for k in range(BLOCKS)], axis=0)
-    for copy in copies[2:]:
+    for copy in copies:
         copy.wait()
-    u_side, u_back = u_ref[...], ut_ref[...]
+    u_side, u_back = weights_of(wrec_ref)
     for l in range(per_block):
         fwd = forward_step(fwd, steps_ref, l, u_side, per_block)
         state_ref.at[0][pl.ds(l, BLOCKS, stride=per_block), :] = fwd
@@ -609,55 +548,37 @@
         gate_bias,
     )
     merge = call(
-        merge_kernel, (shape(1, ROWS, H), shape(6, H + 8, H)), 10**8, "vv", "vv"
+        merge_kernel, (shape(1, ROWS, H), shape(2, H + 8, H)), 10**8, "vv", "vv"
     )
 
     def exchange(packed, groups):
         return lax.all_to_all(packed, "seq", 0, 0, axis_index_groups=groups)
 
-    def pair(packed, bit, flip, copies):
+    def pair(packed, path, bit, flip, copies):
         other = lax.ppermute(packed, "seq", [(i, i ^ flip) for i in range(count)])
         return call(
             functools.partial(pair_kernel, bit=bit),
             (shape(copies, ROWS, H), shape(2, H + 8, H)),
             10**8,
-            "vvv",
+            "vvvv",
             "vv",
-        )(packed, other, recurrent_weight)
-
-    pack, links1 = merge(exchange(pack, near), recurrent_weight)
-    pack, path2 = pair(pack, 4, 7, 1)
-    pack, path3 = pair(pack, 8, 12, 4)
-    group = exchange(pack, far)
-    found = (
-        (2, H, 2 * H),
-        (8, H),
-        (H, 6 * H),
-        (3 * H, 2 * H),
-    )
-    kinds = (BF16, F32, BF16, BF16)
-    buffers = [pltpu.VMEM(dims, kind) for dims, kind in zip(found, kinds)]
-    reached = call(
-        reach_kernel,
-        tuple(jax.ShapeDtypeStruct(dims, kind) for dims, kind in zip(found, kinds)),
-        10**8,
-        "vvvv",
-        "hhhh",
-        buffers + [pltpu.SemaphoreType.DMA((4,))],
-    )(links1, path2, path3, recurrent_weight)
+        )(packed, other, path, recurrent_weight)
+
+    pack, path = merge(exchange(pack, near), recurrent_weight)
+    pack, path = pair(pack, path, 4, 7, 1)
+    pack, path = pair(pack, path, 8, 12, 4)
     new_state, adjoint = call(
         apply_kernel,
         (shape(1, H, H), shape(1, H, H)),
         10**8,
-        "vvvhhhhhh",
+        "vvvvhh",
         "vv",
-        buffers
-        + [
+        [
             pltpu.VMEM((5, H, H), F32),
             pltpu.VMEM((1, H, H), F32),
-            pltpu.SemaphoreType.DMA((6,)),
+            pltpu.SemaphoreType.DMA((2,)),
         ],
-    )(group, nodes, recurrent_weight, *reached, steps, cotangent)
+    )(exchange(pack, far), path, nodes, recurrent_weight, steps, cotangent)
     return new_state, adjoint
 
 

time: 65.9 us -> 64.8 us (0.983)
  blocking collectives: 15.3 us -> 26.4 us
  waiting for transfers between devices: 11.1 us -> 5.84 us
  starting transfers between devices: 23 us -> 18.5 us
  Pallas kernels: 15.5 us -> 13.1 us
    all_to_all x1 -> x2, blocking collectives: 15.3 us -> 26.4 us  [exchange(): return lax.all_to_all(packed, 'seq', 0, 0, axis_index_groups=groups)]
    all_to_all x1 -> x0, waiting for transfers between devices: 5.29 us -> none  [exchange(): return lax.all_to_all(packed, 'seq', 0, 0, axis_index_groups=groups)]
    all_to_all x1 -> x0, starting transfers between devices: 4.47 us -> none  [exchange(): return lax.all_to_all(packed, 'seq', 0, 0, axis_index_groups=groups)]
    pallas_call x6 -> x5, Pallas kernels: 15.5 us -> 13.1 us  [placed(): run(*(pltpu.with_memory_space_constraint(a, pltpu.HBM) if k == 'h' else a...]
  transfers between devices with their start and end apart: 3 -> 2, of which waited for: 3 -> 2; matrix products, arithmetic and copies ran while one was open for 0% -> 0% of each run, Pallas kernels for 2% -> 0%
where the time goes in v6:
time: 64.8 us; the launch traced here: 64.5 us
  blocking collectives  26.4 us (41%)
  starting transfers between devices  18.5 us (29%)
  Pallas kernels  13.1 us (20%)
  waiting for transfers between devices  5.84 us (9%)
  between operations  0.69 us (1%)
    all_to_all x2, blocking collectives, exchange(): return lax.all_to_all(packed, 'seq', 0, 0, axis_index_groups=groups)  26.4 us
    ppermute x2, starting transfers between devices, pair(): other = lax.ppermute(packed, 'seq', [(i, i ^ flip) for i in range(count)])  18.5 us
    pallas_call x5, Pallas kernels, placed(): run(*(pltpu.with_memory_space_constraint(a, pltpu.HBM) if k == 'h' else a...  13.1 us
    ppermute x2, waiting for transfers between devices, pair(): other = lax.ppermute(packed, 'seq', [(i, i ^ flip) for i in range(count)])  5.84 us
  transfers between devices with their start and end apart: 2, of which 2 were waited for; matrix products, arithmetic and copies ran while one was open for 0% of the time, Pallas kernels for 0%

profile of v6, /device:TPU:6, one launch (start us, length us, event | category | flops | bytes accessed | tf_op | source)
XLA Modules:
  0.0 64.5 jit_solution(10834790526997479521)
XLA Ops:
  0.6 0.0 copy-start
  0.6 7.8 %shard_map.86 = (f32[4,144,128]{2,1,0:T(8,128)S(1)}, f32[32,136,128]{2,1,0:T(8,128)S(1)}, f32[5,128,128]{2,1,0:T(8,128)}) custom-call(f32[1,128,128]{2,1,0:T(8,128)} %x_hbm.1, f32[1,128,128]{2,1,0:T(8,128)} %traj_hbm.1, f32[1,128,128]{2,1,0:T(8,128)} %cot_hbm.3, f32[1,128]{1,0:T(1,128)} %init_hbm.1, f32[128,384]{1,0:T(8,128)} %win_hbm.1, ...), custom_call_target="tpu_custom_call" | custom-call | flops 2000000000 | bytes 1048576 | tf_op jit(solution)/shard_map/pallas_call | solution.py:493
  8.4 15.3 %all_to_all.10.group_ref = f32[4,144,128]{2,1,0:T(8,128)S(1)} all-to-all(f32[4,144,128]{2,1,0:T(8,128)S(1)} %get-tuple-element.11), channel_id=1, replica_groups={{0,1,2,3},{4,5,6,7},{8,9,10,11},{12,13,14,15},{16,17,18,19},{20,21,22,2..., dimensions={0} | all-to-all | bytes 589824 | tf_op jit(solution)/shard_map/all_to_all | solution.py:555
  23.7 0.0 copy-done
  23.7 0.9 %shard_map.87 = (f32[1,144,128]{2,1,0:T(8,128)S(1)}, f32[2,136,128]{2,1,0:T(8,128)S(1)}) custom-call(f32[4,144,128]{2,1,0:T(8,128)S(1)} %all_to_all.10.group_ref, f32[128,384]{1,0:T(8,128)S(1)} %copy-done), custom_call_target="tpu_custom_call" | custom-call | flops 100000000 | bytes 1048576 | tf_op jit(solution)/shard_map/pallas_call | solution.py:493
  24.6 10.0 %collective-permute-start = (f32[1,144,128]{2,1,0:T(8,128)S(1)}, f32[1,144,128]{2,1,0:T(8,128)S(1)}, u32[]{:S(2)}, u32[]{:S(2)}) collective-permute-start(f32[1,144,128]{2,1,0:T(8,128)S(1)} %get-tuple-element.12.own_ref), channel_id=1, source_target_pairs={{0,7},{1,6},{2,5},{3,4},{4,3},{5,2},{6,1},{7,0},{8,15},{9,14},{10,... | collective-permute-start | bytes 221192 | tf_op jit(solution)/shard_map/ppermute | solution.py:558
  34.6 2.9 %collective-permute-done.other_ref = f32[1,144,128]{2,1,0:T(8,128)S(1)} collective-permute-done((f32[1,144,128]{2,1,0:T(8,128)S(1)}, f32[1,144,128]{2,1,0:T(8,128)S(1)}, u32[]{:S(2)}, u32[]{:S(2)}) %collective-permute-start) | collective-permute-done | bytes 73760 | tf_op jit(solution)/shard_map/ppermute | solution.py:558
  37.5 0.4 shard_map.88
  38.0 8.5 %collective-permute-start.1 = (f32[1,144,128]{2,1,0:T(8,128)S(1)}, f32[1,144,128]{2,1,0:T(8,128)S(1)}, u32[]{:S(2)}, u32[]{:S(2)}) collective-permute-start(f32[1,144,128]{2,1,0:T(8,128)S(1)} %get-tuple-element.14.own_ref), channel_id=1, source_target_pairs={{0,12},{1,13},{2,14},{3,15},{4,8},{5,9},{6,10},{7,11},{8,4},{9,5},... | collective-permute-start | bytes 221192 | tf_op jit(solution)/shard_map/ppermute | solution.py:558
  46.5 2.9 %collective-permute-done.1.other_ref = f32[1,144,128]{2,1,0:T(8,128)S(1)} collective-permute-done((f32[1,144,128]{2,1,0:T(8,128)S(1)}, f32[1,144,128]{2,1,0:T(8,128)S(1)}, u32[]{:S(2)}, u32[]{:S(2)}) %collective-permute-start.1) | collective-permute-done | bytes 73760 | tf_op jit(solution)/shard_map/ppermute | solution.py:558
  49.5 0.4 shard_map.89
  49.9 11.1 %all_to_all.11.group_ref = f32[4,144,128]{2,1,0:T(8,128)S(1)} all-to-all(f32[4,144,128]{2,1,0:T(8,128)S(1)} %get-tuple-element.16), channel_id=1, replica_groups={{0,16,32,48},{1,17,33,49},{2,18,34,50},{3,19,35,51},{4,20,36,52},{5,21,..., dimensions={0} | all-to-all | bytes 589824 | tf_op jit(solution)/shard_map/all_to_all | solution.py:555
  61.0 3.5 %shard_map.90 = (f32[1,128,128]{2,1,0:T(8,128)}, f32[1,128,128]{2,1,0:T(8,128)}) custom-call(f32[4,144,128]{2,1,0:T(8,128)S(1)} %all_to_all.11.group_ref, f32[2,136,128]{2,1,0:T(8,128)S(1)} %get-tuple-element.17.path_ref, f32[32,136,128]{2,1,0:T(8,128)S(1)} %get-tuple-element.18.nodes_ref, f32[128,384]{1,0:T(8,128)S(1)} %copy-done, ...), custom_call_target="tpu_custom_call" | custom-call | flops 100000000 | bytes 1048576 | tf_op jit(solution)/shard_map/pallas_call | solution.py:493
Async XLA Ops:
  0.6 23.1 %copy-start = (f32[128,384]{1,0:T(8,128)S(1)}, f32[128,384]{1,0:T(8,128)}, u32[]{:S(2)}) copy-start(f32[128,384]{1,0:T(8,128)} %wrec_ref.7) | copy-start | bytes 589828
  24.6 12.9 %collective-permute-start = (f32[1,144,128]{2,1,0:T(8,128)S(1)}, f32[1,144,128]{2,1,0:T(8,128)S(1)}, u32[]{:S(2)}, u32[]{:S(2)}) collective-permute-start(f32[1,144,128]{2,1,0:T(8,128)S(1)} %get-tuple-element.12.own_ref), channel_id=1, source_target_pairs={{0,7},{1,6},{2,5},{3,4},{4,3},{5,2},{6,1},{7,0},{8,15},{9,14},{10,... | collective-permute-start | bytes 221192 | tf_op jit(solution)/shard_map/ppermute | solution.py:558
  38.0 11.5 %collective-permute-start.1 = (f32[1,144,128]{2,1,0:T(8,128)S(1)}, f32[1,144,128]{2,1,0:T(8,128)S(1)}, u32[]{:S(2)}, u32[]{:S(2)}) collective-permute-start(f32[1,144,128]{2,1,0:T(8,128)S(1)} %get-tuple-element.14.own_ref), channel_id=1, source_target_pairs={{0,12},{1,13},{2,14},{3,15},{4,8},{5,9},{6,10},{7,11},{8,4},{9,5},... | collective-permute-start | bytes 221192 | tf_op jit(solution)/shard_map/ppermute | solution.py:558

commit v7 on v6

--- a/solution.py
+++ b/solution.py
@@ -153,12 +153,11 @@
         copy.wait()
     traj = traj_ref[0]
     rec_in = jnp.concatenate([traj, pad8(init_ref[...])], axis=0)
-    rec_all = jnp.dot(
-        rec_in, wrec_ref[...], precision=lax.Precision.HIGHEST, preferred_element_type=F32
-    )
+    u_side, u_back = weights_of(wrec_ref)
+    rec_all = few_rows(rec_in, u_side)
     rec_init = rec_all[H : H + 1]
     rec_rows = rec_all[:H]
-    for copy in copies[3:]:
+    for copy in copies[3:6]:
         copy.wait()
     proj = (
         jnp.dot(x_ref[0], win_ref[...], precision=lax.Precision.HIGHEST, preferred_element_type=F32)
@@ -175,10 +174,10 @@
         steps_ref[p] = rows
     save = pltpu.make_async_copy(steps_ref, steps_hbm, sems.at[7])
     save.start()
+    copies[6].wait()
 
     ident = eye()
     per_block = H // BLOCKS
-    u_side, u_back = weights_of(wrec_ref)
 
     def some_pairs(k, carry):
         fwd, bwd = carry

time: 64.8 us -> 64.9 us (level)
  no operation moved by 1% of the time
where the time goes in v7:
time: 64.9 us; the launch traced here: 64.7 us
  blocking collectives  26.4 us (41%)
  starting transfers between devices  18.5 us (29%)
  Pallas kernels  13.2 us (20%)
  waiting for transfers between devices  5.85 us (9%)
  between operations  0.69 us (1%)
    all_to_all x2, blocking collectives, exchange(): return lax.all_to_all(packed, 'seq', 0, 0, axis_index_groups=groups)  26.4 us
    ppermute x2, starting transfers between devices, pair(): other = lax.ppermute(packed, 'seq', [(i, i ^ flip) for i in range(count)])  18.5 us
    pallas_call x5, Pallas kernels, placed(): run(*(pltpu.with_memory_space_constraint(a, pltpu.HBM) if k == 'h' else a...  13.2 us
    ppermute x2, waiting for transfers between devices, pair(): other = lax.ppermute(packed, 'seq', [(i, i ^ flip) for i in range(count)])  5.85 us
  transfers between devices with their start and end apart: 2, of which 2 were waited for; matrix products, arithmetic and copies ran while one was open for 0% of the time, Pallas kernels for 0%

profile of v7, /device:TPU:6, one launch (start us, length us, event | category | flops | bytes accessed | tf_op | source)
XLA Modules:
  0.0 64.7 jit_solution(4347461021605469340)
XLA Ops:
  0.6 0.0 copy-start
  0.6 7.9 %shard_map.86 = (f32[4,144,128]{2,1,0:T(8,128)S(1)}, f32[32,136,128]{2,1,0:T(8,128)S(1)}, f32[5,128,128]{2,1,0:T(8,128)}) custom-call(f32[1,128,128]{2,1,0:T(8,128)} %x_hbm.1, f32[1,128,128]{2,1,0:T(8,128)} %traj_hbm.1, f32[1,128,128]{2,1,0:T(8,128)} %cot_hbm.3, f32[1,128]{1,0:T(1,128)} %init_hbm.1, f32[128,384]{1,0:T(8,128)} %win_hbm.1, ...), custom_call_target="tpu_custom_call" | custom-call | flops 2000000000 | bytes 1048576 | tf_op jit(solution)/shard_map/pallas_call | solution.py:492
  8.6 15.3 %all_to_all.10.group_ref = f32[4,144,128]{2,1,0:T(8,128)S(1)} all-to-all(f32[4,144,128]{2,1,0:T(8,128)S(1)} %get-tuple-element.11), channel_id=1, replica_groups={{0,1,2,3},{4,5,6,7},{8,9,10,11},{12,13,14,15},{16,17,18,19},{20,21,22,2..., dimensions={0} | all-to-all | bytes 589824 | tf_op jit(solution)/shard_map/all_to_all | solution.py:554
  23.8 0.0 copy-done
  23.8 0.9 %shard_map.87 = (f32[1,144,128]{2,1,0:T(8,128)S(1)}, f32[2,136,128]{2,1,0:T(8,128)S(1)}) custom-call(f32[4,144,128]{2,1,0:T(8,128)S(1)} %all_to_all.10.group_ref, f32[128,384]{1,0:T(8,128)S(1)} %copy-done), custom_call_target="tpu_custom_call" | custom-call | flops 100000000 | bytes 1048576 | tf_op jit(solution)/shard_map/pallas_call | solution.py:492
  24.8 10.0 %collective-permute-start = (f32[1,144,128]{2,1,0:T(8,128)S(1)}, f32[1,144,128]{2,1,0:T(8,128)S(1)}, u32[]{:S(2)}, u32[]{:S(2)}) collective-permute-start(f32[1,144,128]{2,1,0:T(8,128)S(1)} %get-tuple-element.12.own_ref), channel_id=1, source_target_pairs={{0,7},{1,6},{2,5},{3,4},{4,3},{5,2},{6,1},{7,0},{8,15},{9,14},{10,... | collective-permute-start | bytes 221192 | tf_op jit(solution)/shard_map/ppermute | solution.py:557
  34.8 2.9 %collective-permute-done.other_ref = f32[1,144,128]{2,1,0:T(8,128)S(1)} collective-permute-done((f32[1,144,128]{2,1,0:T(8,128)S(1)}, f32[1,144,128]{2,1,0:T(8,128)S(1)}, u32[]{:S(2)}, u32[]{:S(2)}) %collective-permute-start) | collective-permute-done | bytes 73760 | tf_op jit(solution)/shard_map/ppermute | solution.py:557
  37.7 0.4 shard_map.88
  38.1 8.5 %collective-permute-start.1 = (f32[1,144,128]{2,1,0:T(8,128)S(1)}, f32[1,144,128]{2,1,0:T(8,128)S(1)}, u32[]{:S(2)}, u32[]{:S(2)}) collective-permute-start(f32[1,144,128]{2,1,0:T(8,128)S(1)} %get-tuple-element.14.own_ref), channel_id=1, source_target_pairs={{0,12},{1,13},{2,14},{3,15},{4,8},{5,9},{6,10},{7,11},{8,4},{9,5},... | collective-permute-start | bytes 221192 | tf_op jit(solution)/shard_map/ppermute | solution.py:557
  46.7 2.9 %collective-permute-done.1.other_ref = f32[1,144,128]{2,1,0:T(8,128)S(1)} collective-permute-done((f32[1,144,128]{2,1,0:T(8,128)S(1)}, f32[1,144,128]{2,1,0:T(8,128)S(1)}, u32[]{:S(2)}, u32[]{:S(2)}) %collective-permute-start.1) | collective-permute-done | bytes 73760 | tf_op jit(solution)/shard_map/ppermute | solution.py:557
  49.6 0.4 shard_map.89
  50.0 11.1 %all_to_all.11.group_ref = f32[4,144,128]{2,1,0:T(8,128)S(1)} all-to-all(f32[4,144,128]{2,1,0:T(8,128)S(1)} %get-tuple-element.16), channel_id=1, replica_groups={{0,16,32,48},{1,17,33,49},{2,18,34,50},{3,19,35,51},{4,20,36,52},{5,21,..., dimensions={0} | all-to-all | bytes 589824 | tf_op jit(solution)/shard_map/all_to_all | solution.py:554
  61.1 3.5 %shard_map.90 = (f32[1,128,128]{2,1,0:T(8,128)}, f32[1,128,128]{2,1,0:T(8,128)}) custom-call(f32[4,144,128]{2,1,0:T(8,128)S(1)} %all_to_all.11.group_ref, f32[2,136,128]{2,1,0:T(8,128)S(1)} %get-tuple-element.17.path_ref, f32[32,136,128]{2,1,0:T(8,128)S(1)} %get-tuple-element.18.nodes_ref, f32[128,384]{1,0:T(8,128)S(1)} %copy-done, ...), custom_call_target="tpu_custom_call" | custom-call | flops 100000000 | bytes 1048576 | tf_op jit(solution)/shard_map/pallas_call | solution.py:492
Async XLA Ops:
  0.6 23.2 %copy-start = (f32[128,384]{1,0:T(8,128)S(1)}, f32[128,384]{1,0:T(8,128)}, u32[]{:S(2)}) copy-start(f32[128,384]{1,0:T(8,128)} %wrec_ref.7) | copy-start | bytes 589828
  24.8 12.9 %collective-permute-start = (f32[1,144,128]{2,1,0:T(8,128)S(1)}, f32[1,144,128]{2,1,0:T(8,128)S(1)}, u32[]{:S(2)}, u32[]{:S(2)}) collective-permute-start(f32[1,144,128]{2,1,0:T(8,128)S(1)} %get-tuple-element.12.own_ref), channel_id=1, source_target_pairs={{0,7},{1,6},{2,5},{3,4},{4,3},{5,2},{6,1},{7,0},{8,15},{9,14},{10,... | collective-permute-start | bytes 221192 | tf_op jit(solution)/shard_map/ppermute | solution.py:557
  38.1 11.5 %collective-permute-start.1 = (f32[1,144,128]{2,1,0:T(8,128)S(1)}, f32[1,144,128]{2,1,0:T(8,128)S(1)}, u32[]{:S(2)}, u32[]{:S(2)}) collective-permute-start(f32[1,144,128]{2,1,0:T(8,128)S(1)} %get-tuple-element.14.own_ref), channel_id=1, source_target_pairs={{0,12},{1,13},{2,14},{3,15},{4,8},{5,9},{6,10},{7,11},{8,4},{9,5},... | collective-permute-start | bytes 221192 | tf_op jit(solution)/shard_map/ppermute | solution.py:557
